TPU v7x, 128 devices: a whole 4x4x4 slice. The times are simulated.
128 devices in a mesh: prow: 32 (over x, z_lo, y), pcol: 4 (over z_hi, core).
Axes of the slice: x: 4, y: 4, z: 4 (z_hi: 2, z_lo: 2; z = z_hi * 2 + z_lo), core: 2. Of those that a mesh axis runs over, the one named last changes fastest.
Arguments:
- inverse_band: float32 [4096, 4096], P('prow', 'pcol'), may hold values from -0.09375 to 0.09375
- factor_panel: float32 [2, 4096, 512], P(None, 'prow', 'pcol'), may hold values from -0.6 to 0.6
- diag_inverse: float32 [2, 512, 512], replicated, may hold values from -1 to 2, as said below
- ancestors: int32 [2, 63], replicated, may hold values from 0 to 63, as said below
- counts: int32 [2], replicated, may hold values from 1 to 63, as said below
Outputs:
- new_column: float32 [2, 4096, 512], P(None, 'prow', 'pcol')
- diag_block: float32 [2, 512, 512], P(None, 'prow', 'pcol')
Inputs may be any that keep to these rules, and one draw needn't show every extreme that they name: Each row holds distinct block numbers; its first counts[s] entries are in increasing order and include 63; the entries after them are other block numbers, which are not ancestors. One of the two counts is 63; the other is below 63. `diag_inverse`: lower triangular; diagonal entries from 0.5 to 2.
All inputs are finite; a program needn't handle non-finite values.
Results may differ from a plain program's by a relative error of at most 0.000073.
Values sent between devices are 32-bit elements; how exact they have to be, the bound alone decides.
No kernel may reach another device: no remote copies, remote signals or barrier semaphores. Data moves between devices by JAX's collectives and lax.ppermute only.
A program may use at most 64 MiB of HBM per device.

v0:
```python
import jax
import jax.numpy as jnp
import numpy as np
from jax import lax
from jax.experimental import pallas as pl
from jax.experimental.pallas import tpu as pltpu
from jax.sharding import Mesh, PartitionSpec as P


W = 512
BS = 64
Q = 128
AXES = ("x", "zl", "y", "zh", "core")
SIZES = (4, 2, 4, 2, 2)
PROW = ("x", "zl", "y")
PCOL = ("zh", "core")

SWAP = [(0, 1), (1, 0)]
EVEN = [(0, 1), (1, 0), (2, 3), (3, 2)]
ODD = [(0, 3), (3, 0), (1, 2), (2, 1)]
ALL_VMEM = pl.BlockSpec(memory_space=pltpu.VMEM)


def route(where):
    pairs = []
    for source in np.ndindex(*SIZES):
        x, zl, y, zh, core = source
        target = where(x, zl, y, 2 * zh + core)
        tx, tzl, ty, tc = target
        pairs.append(
            (
                int(np.ravel_multi_index(source, SIZES)),
                int(np.ravel_multi_index((tx, tzl, ty, tc // 2, tc % 2), SIZES)),
            )
        )
    return pairs


def pick(x, i, dim):
    return lax.dynamic_index_in_dim(x, i, dim, keepdims=False)


def split(v):
    high = v.astype(jnp.bfloat16)
    return high, (v - high.astype(jnp.float32)).astype(jnp.bfloat16)


def dot3(left, right):
    ah, al = left
    bh, bl = right

    def one(a, b):
        return jnp.dot(a, b, preferred_element_type=jnp.float32)

    return one(ah, bh) + (one(ah, bl) + one(al, bh))


def position():
    return [lax.axis_index(name) for name in AXES]


def call(body, out_shape, arrays, limit, in_specs=None, scratch=()):
    return pl.pallas_call(
        body,
        out_shape=out_shape,
        in_specs=in_specs or [ALL_VMEM] * len(arrays),
        out_specs=(ALL_VMEM,) * len(out_shape),
        scratch_shapes=scratch,
        compiler_params=pltpu.CompilerParams(vmem_limit_bytes=limit * 1024 * 1024),
    )(*arrays)


def early(counts_hbm, ancestors_hbm, diag, square, col_mask, row_mask, out_mask, tile, counts, ancestors, sems):
    x, zl, y, zh, core = position()
    prow = 8 * x + 4 * zl + y
    pcol = 2 * zh + core
    fetch = [
        pltpu.make_async_copy(counts_hbm, counts, sems.at[0]),
        pltpu.make_async_copy(ancestors_hbm, ancestors, sems.at[1]),
    ]
    for copy in fetch:
        copy.start()
    for s in range(2):
        left = diag[s, :, pl.ds(pl.multiple_of((prow // 8) * Q, Q), Q)]
        right = diag[s, :, pl.ds(pl.multiple_of(pcol * Q, Q), Q)]
        tile[...] = dot3(split(left.T), split(right))
        square[s] = tile[pl.ds(pl.multiple_of((prow % 8) * 16, 16), 16), :]
    for copy in fetch:
        copy.wait()
    lane = lax.broadcasted_iota(jnp.int32, (32, 63), 1)
    slot = lax.broadcasted_iota(jnp.int32, (32, 63), 0)
    row_group = jnp.where(slot < 18, prow, prow + 4 - 8 * zl)
    block = jnp.where(slot < 16, (slot // 2) * 4 + pcol, row_group) + (slot % 2) * 32
    found = []
    for s in range(2):
        hit = (ancestors[s : s + 1, :] == block) & (lane < counts[s])
        found.append(jnp.max(hit.astype(jnp.float32), axis=1, keepdims=True))
        for j in range(2):
            out_mask[s, j * BS : (j + 1) * BS, :] = jnp.broadcast_to(found[s][16 + j : 17 + j, :], (BS, Q))
    owned = jnp.where(zl == 0, found[0], found[1])
    column = lax.broadcasted_iota(jnp.int32, (1, 8 * Q), 1) // BS
    mask = jnp.zeros((1, 8 * Q), jnp.float32)
    for j in range(16):
        mask = jnp.where(column == j, owned[j : j + 1, :], mask)
    col_mask[...] = mask
    for j in range(4):
        row_mask[j * BS : (j + 1) * BS, :] = jnp.broadcast_to(owned[16 + j : 17 + j, :], (BS, Q))


def left_factor(diag, row_mask, mine, g_zl, g_core, g_zh, hi_t, lo_t):
    _, zl, _, zh, core = position()
    pcol = 2 * zh + core
    quarters = (
        (mine[...], g_zl[...], pcol),
        (g_core[0], g_core[1], 2 * zh + 1 - core),
        (g_zh[0, 0], g_zh[0, 1], 2 - 2 * zh + core),
        (g_zh[1, 0], g_zh[1, 1], 3 - 2 * zh - core),
    )
    scaled = jnp.zeros((2 * Q, W), jnp.float32)
    for own, partner, quarter in quarters:
        rows = jnp.concatenate([own, partner], axis=0) * row_mask[...]
        start = pl.multiple_of(quarter * Q, Q)
        scaled = scaled + dot3(split(rows), split(diag[zl, pl.ds(start, Q), :]))
    hi, lo = split(scaled.T)
    hi_t[...] = hi
    lo_t[...] = lo


def products(
    band_own,
    band_other,
    col_mask,
    a1,
    a1r,
    a2,
    a2r,
    b1,
    b1r,
    b2,
    b2r,
    diag,
    part_keep,
    part_send,
    band_hi,
    band_lo,
    panel_hi,
    panel_lo,
    diag_hi,
    diag_lo,
):
    x, zl, y, zh, core = position()
    pieces = {}
    for ref, qs in ((a1, (0, 1)), (a1r, (3, 2))):
        for i, q in enumerate(qs):
            for j, xo in enumerate((0, 1)):
                pieces[0, xo, q] = (ref, i, j)
    for ref, qs in ((a2, (0, 3)), (a2r, (1, 2))):
        for i, q in enumerate(qs):
            for j, xo in enumerate((3, 2)):
                pieces[0, xo, q] = (ref, i, j)
    for ref, xs in ((b1, (0, 1)), (b1r, (3, 2))):
        for i, xo in enumerate(xs):
            for j, q in enumerate((0, 1)):
                pieces[1, xo, q] = (ref, i, j)
    for ref, xs in ((b2, (0, 3)), (b2r, (1, 2))):
        for i, xo in enumerate(xs):
            for j, q in enumerate((3, 2)):
                pieces[1, xo, q] = (ref, i, j)
    for (stream, xo, q), (ref, i, j) in pieces.items():
        hi, lo = split(ref[i, j])
        rows = slice((2 * xo + stream) * Q, (2 * xo + stream + 1) * Q)
        cols = slice(q * Q, (q + 1) * Q)
        panel_hi[rows, cols] = hi
        panel_lo[rows, cols] = lo
    for xo in range(4):
        for stream in range(2):
            side = zl if stream == 0 else 1 - zl
            start = pl.multiple_of((x ^ xo) * (2 * Q) + side * Q, Q)
            mask = col_mask[:, pl.ds(start, Q)]
            cols = slice((2 * xo + stream) * Q, (2 * xo + stream + 1) * Q)
            for r, ref in enumerate((band_own, band_other)):
                hi, lo = split(ref[:, pl.ds(start, Q)] * mask)
                band_hi[r * Q : (r + 1) * Q, cols] = hi
                band_lo[r * Q : (r + 1) * Q, cols] = lo
    for q in range(4):
        start = pl.multiple_of((y ^ q) * Q, Q)
        hi, lo = split(diag[zl, pl.ds(start, Q), :])
        diag_hi[q * Q : (q + 1) * Q, :] = hi
        diag_lo[q * Q : (q + 1) * Q, :] = lo
    product = dot3((band_hi[...], band_lo[...]), (panel_hi[...], panel_lo[...]))
    partial = dot3(split(product), (diag_hi[...], diag_lo[...]))
    for c in range(2):

        @pl.when(core == c)
        def _():
            for h in range(2):
                side = jnp.where(zh == h, 0, 1)
                for ref, k in ((part_keep, c), (part_send, 1 - c)):
                    part = partial[:, (2 * h + k) * Q : (2 * h + k + 1) * Q]
                    ref[:, side] = part.reshape(2, Q, Q)


def correction(part_keep, part_got, left_hi, left_lo, part, corr):
    _, _, _, zh, _ = position()
    part[...] = part_keep[...] + part_got[...]
    right = jnp.concatenate(
        [jnp.concatenate([part[0, s], part[1, s]], axis=0) for s in range(2)], axis=1
    )
    value = dot3((left_hi[...], left_lo[...]), split(right))
    corr[:, zh] = value[:, :Q].reshape(32, 16, Q)
    corr[:, 1 - zh] = value[:, Q:].reshape(32, 16, Q)


def f32(*shape):
    return jax.ShapeDtypeStruct(shape, jnp.float32)


def bf16(*shape):
    return jax.ShapeDtypeStruct(shape, jnp.bfloat16)


def vmem(*shapes):
    return [pltpu.VMEM(shape, jnp.bfloat16) for shape in shapes]


def step(band, panel, diag_inverse, ancestors, counts):
    zl = lax.axis_index("zl")
    mine = pick(panel, zl, 0)
    other = pick(panel, 1 - zl, 0)
    a_here = lax.ppermute(mine, AXES, route(lambda x, zl, y, c: (x, zl, c, y)))
    b_here = lax.ppermute(other, AXES, route(lambda x, zl, y, c: (x, 1 - zl, c, y)))
    band_other = lax.ppermute(band, "zl", SWAP)

    square, col_mask, row_mask, out_mask = call(
        early,
        (f32(2, 16, Q), f32(1, 8 * Q), f32(2 * Q, Q), f32(2, Q, Q)),
        (counts, ancestors, diag_inverse),
        12,
        in_specs=[pl.BlockSpec(memory_space=pl.ANY)] * 2 + [ALL_VMEM],
        scratch=[
            pltpu.VMEM((Q, Q), jnp.float32),
            pltpu.SMEM((2,), jnp.int32),
            pltpu.VMEM((2, 63), jnp.int32),
            pltpu.SemaphoreType.DMA((2,)),
        ],
    )
    a12 = jnp.stack([a_here, lax.ppermute(a_here, "x", EVEN)])
    b12 = jnp.stack([b_here, lax.ppermute(b_here, "y", EVEN)])
    a34 = lax.ppermute(a12, "x", ODD)
    b34 = lax.ppermute(b12, "y", ODD)
    a1 = jnp.stack([a12, lax.ppermute(a12, "y", EVEN)])
    b1 = jnp.stack([b12, lax.ppermute(b12, "x", EVEN)])
    a2 = jnp.stack([a34, lax.ppermute(a34, "y", ODD)])
    b2 = jnp.stack([b34, lax.ppermute(b34, "x", ODD)])
    a1r = lax.ppermute(a1, "y", ODD)
    b1r = lax.ppermute(b1, "x", ODD)
    a2r = lax.ppermute(a2, "y", EVEN)
    b2r = lax.ppermute(b2, "x", EVEN)

    g_zl = lax.ppermute(other, "zl", SWAP)
    rows = jnp.stack([mine, g_zl])
    g_core = lax.ppermute(rows, "core", SWAP)
    g_zh = lax.ppermute(jnp.stack([rows, g_core]), "zh", SWAP)
    left_hi, left_lo = call(
        left_factor,
        (bf16(W, 2 * Q), bf16(W, 2 * Q)),
        (diag_inverse, row_mask, mine, g_zl, g_core, g_zh),
        12,
    )
    part_keep, part_send = call(
        products,
        (f32(2, 2, Q, Q), f32(2, 2, Q, Q)),
        (band, band_other, col_mask, a1, a1r, a2, a2r, b1, b1r, b2, b2r, diag_inverse),
        20,
        scratch=vmem(*[(2 * Q, 8 * Q)] * 2, *[(8 * Q, W)] * 2, *[(W, W)] * 2),
    )
    part_got = lax.ppermute(part_send, "core", SWAP)
    parts, corr = call(
        correction,
        (f32(2, 2, Q, Q), f32(32, 2, 16, Q)),
        (part_keep, part_got, left_hi, left_lo),
        12,
    )
    landed = lax.all_to_all(corr.reshape(64, 16, Q), ("x", "zl", "y", "zh"), 0, 0, tiled=True)
    in_a = lax.ppermute(parts[0, 1], "zh", SWAP)
    in_b = lax.ppermute(parts[1, 0], "zl", SWAP)
    in_c = lax.ppermute(parts[1, 1], ("zl", "zh"), [(0, 3), (1, 2), (2, 1), (3, 0)])
    own_sum = parts[0, 0] + in_a
    other_sum = in_b + in_c
    summed = jnp.stack(
        [jnp.where(zl == 0, own_sum, other_sum), jnp.where(zl == 0, other_sum, own_sum)]
    )
    new_column = -(summed * out_mask)
    reduced = landed.reshape(4, 2, 8, 16, Q).sum(axis=(0, 2))
    return (new_column, square + reduced)


def solution(mesh):
    fine = Mesh(mesh.devices.reshape(SIZES), AXES)
    in_specs = (P(PROW, PCOL), P(None, PROW, PCOL), P(), P(), P())
    out_specs = (P(None, PROW, PCOL), P(None, PROW, PCOL))
    return jax.shard_map(step, mesh=fine, in_specs=in_specs, out_specs=out_specs, check_vma=False)
```

profile of v0, /device:TPU:0, one launch (start us, length us, event | category | flops | bytes accessed | tf_op | source)
XLA Modules:
  0.0 73.7 jit_solution(2952630119293288835)
XLA Ops:
  0.7 1.0 %dynamic-slice_bitcast_fusion = (f32[128,128]{1,0:T(8,128)S(1)}, f32[1,128,128]{2,1,0:T(8,128)S(1)}) fusion(f32[2,128,128]{2,1,0:T(8,128)} %param.6, s32[]{:T(128)S(6)} %select_n.21, s32[]{:T(128)S(6)} %select_n.20), kind=kLoop, calls=%fused_computation.16 | loop fusion | bytes 262152 | tf_op jit(solution)/shard_map/jit(dynamic_index_in_dim)/squeeze | solution.py:40
  1.7 2.1 %collective-permute-start.8 = (f32[128,128]{1,0:T(8,128)S(1)}, f32[128,128]{1,0:T(8,128)S(1)}, u32[]{:S(2)}, u32[]{:S(2)}) collective-permute-start(f32[128,128]{1,0:T(8,128)S(1)} %get-tuple-element.31), channel_id=1, source_target_pairs={{0,16},{1,20},{2,24},{3,28},{4,17},{5,21},{6,25},{7,29},{8,18},{9,... | collective-permute-start | bytes 196616 | tf_op jit(solution)/shard_map/ppermute | solution.py:231
  4.5 1.9 %collective-permute-done.8 = f32[128,128]{1,0:T(8,128)S(1)} collective-permute-done((f32[128,128]{1,0:T(8,128)S(1)}, f32[128,128]{1,0:T(8,128)S(1)}, u32[]{:S(2)}, u32[]{:S(2)}) %collective-permute-start.8) | collective-permute-done | bytes 65568 | tf_op jit(solution)/shard_map/ppermute | solution.py:231
  6.3 2.2 %collective-permute-start.9 = (f32[128,128]{1,0:T(8,128)S(1)}, f32[128,128]{1,0:T(8,128)S(1)}, u32[]{:S(2)}, u32[]{:S(2)}) collective-permute-start(f32[128,128]{1,0:T(8,128)S(1)} %collective-permute-done.8), channel_id=1, source_target_pairs={{0,4},{4,0},{8,12},{12,8},{1,5},{5,1},{9,13},{13,9},{2,6},{6,2},{1... | collective-permute-start | bytes 196616 | tf_op jit(solution)/shard_map/ppermute | solution.py:248
  8.6 1.4 %collective-permute-start.16 = (f32[128,128]{1,0:T(8,128)S(1)}, f32[128,128]{1,0:T(8,128)S(1)}, u32[]{:S(2)}, u32[]{:S(2)}) collective-permute-start(f32[128,128]{1,0:T(8,128)S(1)} %get-tuple-element.31), channel_id=1, source_target_pairs={{0,16},{16,0},{1,17},{17,1},{2,18},{18,2},{3,19},{19,3},{4,20},{20... | collective-permute-start | bytes 196616 | tf_op jit(solution)/shard_map/ppermute | solution.py:260
  10.6 1.5 %collective-permute-start.2 = (f32[128,128]{1,0:T(8,128)S(1)}, f32[128,128]{1,0:T(8,128)S(1)}, u32[]{:S(2)}, u32[]{:S(2)}) collective-permute-start(f32[128,128]{1,0:T(8,128)S(1)} %collective-permute-done.1), channel_id=1, source_target_pairs={{0,32},{32,0},{64,96},{96,64},{1,33},{33,1},{65,97},{97,65},{2,34}... | collective-permute-start | bytes 196616 | tf_op jit(solution)/shard_map/ppermute | solution.py:247
  12.1 6.8 %collective-permute-start.12 = (f32[2,128,128]{2,1,0:T(8,128)S(1)}, f32[2,128,128]{2,1,0:T(8,128)S(1)}, u32[]{:S(2)}, u32[]{:S(2)}) collective-permute-start(f32[2,128,128]{2,1,0:T(8,128)S(1)} %get-tuple-element.30), channel_id=1, source_target_pairs={{0,12},{12,0},{4,8},{8,4},{1,13},{13,1},{5,9},{9,5},{2,14},{14,2},... | collective-permute-start | bytes 393224 | tf_op jit(solution)/shard_map/ppermute | solution.py:250
  19.5 2.8 %collective-permute-start.5 = (f32[2,128,128]{2,1,0:T(8,128)S(1)}, f32[2,128,128]{2,1,0:T(8,128)S(1)}, u32[]{:S(2)}, u32[]{:S(2)}) collective-permute-start(f32[2,128,128]{2,1,0:T(8,128)S(1)} %get-tuple-element.34), channel_id=1, source_target_pairs={{0,96},{96,0},{32,64},{64,32},{1,97},{97,1},{33,65},{65,33},{2,98}... | collective-permute-start | bytes 393224 | tf_op jit(solution)/shard_map/ppermute | solution.py:249
  22.3 2.3 %collective-permute-start.3 = (f32[2,128,128]{2,1,0:T(8,128)S(1)}, f32[2,128,128]{2,1,0:T(8,128)S(1)}, u32[]{:S(2)}, u32[]{:S(2)}) collective-permute-start(f32[2,128,128]{2,1,0:T(8,128)S(1)} %get-tuple-element.34), channel_id=1, source_target_pairs={{0,4},{4,0},{8,12},{12,8},{1,5},{5,1},{9,13},{13,9},{2,6},{6,2},{1... | collective-permute-start | bytes 393224 | tf_op jit(solution)/shard_map/ppermute | solution.py:251
  24.7 1.9 %collective-permute-start.13 = (f32[2,128,128]{2,1,0:T(8,128)S(1)}, f32[2,128,128]{2,1,0:T(8,128)S(1)}, u32[]{:S(2)}, u32[]{:S(2)}) collective-permute-start(f32[2,128,128]{2,1,0:T(8,128)S(1)} %collective-permute-done.12), channel_id=1, source_target_pairs={{0,96},{96,0},{32,64},{64,32},{1,97},{97,1},{33,65},{65,33},{2,98}... | collective-permute-start | bytes 393224 | tf_op jit(solution)/shard_map/ppermute | solution.py:254
  26.6 2.2 %collective-permute-start.11 = (f32[2,2,128,128]{3,2,1,0:T(8,128)S(1)}, f32[2,2,128,128]{3,2,1,0:T(8,128)S(1)}, u32[]{:S(2)}, u32[]{:S(2)}) collective-permute-start(f32[2,2,128,128]{3,2,1,0:T(8,128)S(1)} %pad_maximum_fusion.2.b1), channel_id=1, source_target_pairs={{0,96},{96,0},{32,64},{64,32},{1,97},{97,1},{33,65},{65,33},{2,98}... | collective-permute-start | bytes 786440 | tf_op jit(solution)/shard_map/ppermute | solution.py:256
  28.8 2.6 %collective-permute-start.6 = (f32[2,128,128]{2,1,0:T(8,128)S(1)}, f32[2,128,128]{2,1,0:T(8,128)S(1)}, u32[]{:S(2)}, u32[]{:S(2)}) collective-permute-start(f32[2,128,128]{2,1,0:T(8,128)S(1)} %collective-permute-done.5), channel_id=1, source_target_pairs={{0,12},{12,0},{4,8},{8,4},{1,13},{13,1},{5,9},{9,5},{2,14},{14,2},... | collective-permute-start | bytes 393224 | tf_op jit(solution)/shard_map/ppermute | solution.py:253
  32.4 2.7 %collective-permute-start.4 = (f32[2,2,128,128]{3,2,1,0:T(8,128)S(1)}, f32[2,2,128,128]{3,2,1,0:T(8,128)S(1)}, u32[]{:S(2)}, u32[]{:S(2)}) collective-permute-start(f32[2,2,128,128]{3,2,1,0:T(8,128)S(1)} %pad_maximum_fusion.a1), channel_id=1, source_target_pairs={{0,12},{12,0},{4,8},{8,4},{1,13},{13,1},{5,9},{9,5},{2,14},{14,2},... | collective-permute-start | bytes 786440 | tf_op jit(solution)/shard_map/ppermute | solution.py:255
  35.3 2.4 %collective-permute-start.7 = (f32[2,2,128,128]{3,2,1,0:T(8,128)S(1)}, f32[2,2,128,128]{3,2,1,0:T(8,128)S(1)}, u32[]{:S(2)}, u32[]{:S(2)}) collective-permute-start(f32[2,2,128,128]{3,2,1,0:T(8,128)S(1)} %pad_maximum_fusion.1.a2), channel_id=1, source_target_pairs={{0,4},{4,0},{8,12},{12,8},{1,5},{5,1},{9,13},{13,9},{2,6},{6,2},{1... | collective-permute-start | bytes 786440 | tf_op jit(solution)/shard_map/ppermute | solution.py:257
  38.4 2.1 %collective-permute-start.18 = (f32[2,2,128,128]{3,2,1,0:T(8,128)S(1)}, f32[2,2,128,128]{3,2,1,0:T(8,128)S(1)}, u32[]{:S(2)}, u32[]{:S(2)}) collective-permute-start(f32[2,2,128,128]{3,2,1,0:T(8,128)S(1)} %pad_maximum_fusion.4), channel_id=1, source_target_pairs={{0,2},{2,0},{1,3},{3,1},{4,6},{6,4},{5,7},{7,5},{8,10},{10,8},{9,1... | collective-permute-start | bytes 786440 | tf_op jit(solution)/shard_map/ppermute | solution.py:263
  40.8 1.4 %collective-permute-done.14.b2r = f32[2,2,128,128]{3,2,1,0:T(8,128)S(1)} collective-permute-done((f32[2,2,128,128]{3,2,1,0:T(8,128)S(1)}, f32[2,2,128,128]{3,2,1,0:T(8,128)S(1)}, u32[]{:S(2)}, u32[]{:S(2)}) %collective-permute-start.14) | collective-permute-done | bytes 262176 | tf_op jit(solution)/shard_map/ppermute | solution.py:258
  42.3 1.9 %shard_map.69 = (f32[2,2,128,128]{3,2,1,0:T(8,128)S(1)}, f32[2,2,128,128]{3,2,1,0:T(8,128)S(1)}) custom-call(f32[128,1024]{1,0:T(8,128)S(1)} %copy-done.1, f32[128,1024]{1,0:T(8,128)S(1)} %collective-permute-done.band_other, f32[1,1024]{1,0:T(1,128)S(1)} %get-tuple-element.12.col_mask, f32[2,2,128,128]{3,2,1,0:T(8,128)S(1)} %pad_maximum_fusion.a1, ...), custom_call_target="tpu_custom_call" | custom-call | tf_op jit(solution)/shard_map/pallas_call | solution.py:63
  44.3 2.4 %collective-permute-done.18.g_zh = f32[2,2,128,128]{3,2,1,0:T(8,128)S(1)} collective-permute-done((f32[2,2,128,128]{3,2,1,0:T(8,128)S(1)}, f32[2,2,128,128]{3,2,1,0:T(8,128)S(1)}, u32[]{:S(2)}, u32[]{:S(2)}) %collective-permute-start.18) | collective-permute-done | bytes 262176 | tf_op jit(solution)/shard_map/ppermute | solution.py:263
  46.7 1.1 %shard_map.70 = (bf16[512,256]{1,0:T(8,128)(2,1)S(1)}, bf16[512,256]{1,0:T(8,128)(2,1)S(1)}) custom-call(f32[2,512,512]{2,1,0:T(8,128)S(1)} %copy-done, f32[256,128]{1,0:T(8,128)S(1)} %get-tuple-element.15.row_mask, f32[128,128]{1,0:T(8,128)S(1)} %bitcast.40, f32[128,128]{1,0:T(8,128)S(1)} %collective-permute-done.16.g_zl, ...), custom_call_target="tpu_custom_call" | custom-call | tf_op jit(solution)/shard_map/pallas_call | solution.py:63
  47.9 1.2 %shard_map.71 = (f32[2,2,128,128]{3,2,1,0:T(8,128)S(1)}, f32[32,2,16,128]{3,2,1,0:T(8,128)}) custom-call(f32[2,2,128,128]{3,2,1,0:T(8,128)S(1)} %get-tuple-element.13.part_keep, f32[2,2,128,128]{3,2,1,0:T(8,128)S(1)} %collective-permute-done.15.part_got, bf16[512,256]{1,0:T(8,128)(2,1)S(1)} %get-tuple-element.16.left_hi, ...), custom_call_target="tpu_custom_call" | custom-call | tf_op jit(solution)/shard_map/pallas_call | solution.py:63
  49.1 1.8 %collective-permute-start.19 = (f32[128,128]{1,0:T(8,128)S(1)}, f32[128,128]{1,0:T(8,128)S(1)}, u32[]{:S(2)}, u32[]{:S(2)}) collective-permute-start(f32[128,128]{1,0:T(8,128)S(1)} %get-tuple-element.24), channel_id=1, source_target_pairs={{0,2},{2,0},{1,3},{3,1},{4,6},{6,4},{5,7},{7,5},{8,10},{10,8},{9,1... | collective-permute-start | bytes 196616 | tf_op jit(solution)/shard_map/ppermute | solution.py:285
  51.0 2.2 %collective-permute-start.21 = (f32[128,128]{1,0:T(8,128)S(1)}, f32[128,128]{1,0:T(8,128)S(1)}, u32[]{:S(2)}, u32[]{:S(2)}) collective-permute-start(f32[128,128]{1,0:T(8,128)S(1)} %get-tuple-element.25), channel_id=1, source_target_pairs={{0,18},{2,16},{16,2},{18,0},{1,19},{3,17},{17,3},{19,1},{4,22},{6,... | collective-permute-start | bytes 196616 | tf_op jit(solution)/shard_map/ppermute | solution.py:287
  53.2 7.9 %all-to-all-start = ((f32[64,16,128]{2,1,0:T(8,128)}), f32[64,16,128]{2,1,0:T(8,128)S(1)}, u32[]{:S(2)}, u32[]{:S(2)}) async-start(f32[64,16,128]{2,1,0:T(8,128)} %bitcast.23), calls=%async_computation | async-start | bytes 1048576 | tf_op jit(solution)/shard_map/all_to_all | solution.py:284
  61.9 11.1 %all-to-all-done = f32[64,16,128]{2,1,0:T(8,128)S(1)} async-done(((f32[64,16,128]{2,1,0:T(8,128)}), f32[64,16,128]{2,1,0:T(8,128)S(1)}, u32[]{:S(2)}, u32[]{:S(2)}) %all-to-all-start) | async-done | bytes 524320 | tf_op jit(solution)/shard_map/all_to_all | solution.py:284
  (48 shorter events, 5.7 us)
Async XLA Ops:
  0.6 37.1 %copy-start = (f32[2,512,512]{2,1,0:T(8,128)S(1)}, f32[2,512,512]{2,1,0:T(8,128)}, u32[]{:S(2)}) copy-start(f32[2,512,512]{2,1,0:T(8,128)} %diag.5) | copy-start | bytes 6291460
  1.7 4.6 %collective-permute-start.8 = (f32[128,128]{1,0:T(8,128)S(1)}, f32[128,128]{1,0:T(8,128)S(1)}, u32[]{:S(2)}, u32[]{:S(2)}) collective-permute-start(f32[128,128]{1,0:T(8,128)S(1)} %get-tuple-element.31), channel_id=1, source_target_pairs={{0,16},{1,20},{2,24},{3,28},{4,17},{5,21},{6,25},{7,29},{8,18},{9,... | collective-permute-start | bytes 196616 | tf_op jit(solution)/shard_map/ppermute | solution.py:231
  3.8 6.8 %collective-permute-start.1 = (f32[128,128]{1,0:T(8,128)S(1)}, f32[128,128]{1,0:T(8,128)S(1)}, u32[]{:S(2)}, u32[]{:S(2)}) collective-permute-start(f32[128,128]{1,0:T(8,128)S(1)} %bitcast.39), channel_id=1, source_target_pairs={{0,0},{1,4},{2,8},{3,12},{4,1},{5,5},{6,9},{7,13},{8,2},{9,6},{10,... | collective-permute-start | bytes 196616 | tf_op jit(solution)/shard_map/ppermute | solution.py:230
  6.3 5.8 %collective-permute-start.9 = (f32[128,128]{1,0:T(8,128)S(1)}, f32[128,128]{1,0:T(8,128)S(1)}, u32[]{:S(2)}, u32[]{:S(2)}) collective-permute-start(f32[128,128]{1,0:T(8,128)S(1)} %collective-permute-done.8), channel_id=1, source_target_pairs={{0,4},{4,0},{8,12},{12,8},{1,5},{5,1},{9,13},{13,9},{2,6},{6,2},{1... | collective-permute-start | bytes 196616 | tf_op jit(solution)/shard_map/ppermute | solution.py:248
  8.6 13.8 %collective-permute-start.16 = (f32[128,128]{1,0:T(8,128)S(1)}, f32[128,128]{1,0:T(8,128)S(1)}, u32[]{:S(2)}, u32[]{:S(2)}) collective-permute-start(f32[128,128]{1,0:T(8,128)S(1)} %get-tuple-element.31), channel_id=1, source_target_pairs={{0,16},{16,0},{1,17},{17,1},{2,18},{18,2},{3,19},{19,3},{4,20},{20... | collective-permute-start | bytes 196616 | tf_op jit(solution)/shard_map/ppermute | solution.py:260
  10.0 30.9 %collective-permute-start = (f32[128,1024]{1,0:T(8,128)}, f32[128,1024]{1,0:T(8,128)S(1)}, u32[]{:S(2)}, u32[]{:S(2)}) collective-permute-start(f32[128,1024]{1,0:T(8,128)} %band_own.1), channel_id=1, source_target_pairs={{0,16},{16,0},{1,17},{17,1},{2,18},{18,2},{3,19},{19,3},{4,20},{20... | collective-permute-start | bytes 1572872 | tf_op jit(solution)/shard_map/ppermute | solution.py:232
  10.6 8.9 %collective-permute-start.2 = (f32[128,128]{1,0:T(8,128)S(1)}, f32[128,128]{1,0:T(8,128)S(1)}, u32[]{:S(2)}, u32[]{:S(2)}) collective-permute-start(f32[128,128]{1,0:T(8,128)S(1)} %collective-permute-done.1), channel_id=1, source_target_pairs={{0,32},{32,0},{64,96},{96,64},{1,33},{33,1},{65,97},{97,65},{2,34}... | collective-permute-start | bytes 196616 | tf_op jit(solution)/shard_map/ppermute | solution.py:247
  12.1 12.5 %collective-permute-start.12 = (f32[2,128,128]{2,1,0:T(8,128)S(1)}, f32[2,128,128]{2,1,0:T(8,128)S(1)}, u32[]{:S(2)}, u32[]{:S(2)}) collective-permute-start(f32[2,128,128]{2,1,0:T(8,128)S(1)} %get-tuple-element.30), channel_id=1, source_target_pairs={{0,12},{12,0},{4,8},{8,4},{1,13},{13,1},{5,9},{9,5},{2,14},{14,2},... | collective-permute-start | bytes 393224 | tf_op jit(solution)/shard_map/ppermute | solution.py:250
  18.9 5.8 %collective-permute-start.10 = (f32[2,128,128]{2,1,0:T(8,128)S(1)}, f32[2,128,128]{2,1,0:T(8,128)S(1)}, u32[]{:S(2)}, u32[]{:S(2)}) collective-permute-start(f32[2,128,128]{2,1,0:T(8,128)S(1)} %get-tuple-element.30), channel_id=1, source_target_pairs={{0,32},{32,0},{64,96},{96,64},{1,33},{33,1},{65,97},{97,65},{2,34}... | collective-permute-start | bytes 393224 | tf_op jit(solution)/shard_map/ppermute | solution.py:252
  19.5 7.2 %collective-permute-start.5 = (f32[2,128,128]{2,1,0:T(8,128)S(1)}, f32[2,128,128]{2,1,0:T(8,128)S(1)}, u32[]{:S(2)}, u32[]{:S(2)}) collective-permute-start(f32[2,128,128]{2,1,0:T(8,128)S(1)} %get-tuple-element.34), channel_id=1, source_target_pairs={{0,96},{96,0},{32,64},{64,32},{1,97},{97,1},{33,65},{65,33},{2,98}... | collective-permute-start | bytes 393224 | tf_op jit(solution)/shard_map/ppermute | solution.py:249
  22.3 6.5 %collective-permute-start.3 = (f32[2,128,128]{2,1,0:T(8,128)S(1)}, f32[2,128,128]{2,1,0:T(8,128)S(1)}, u32[]{:S(2)}, u32[]{:S(2)}) collective-permute-start(f32[2,128,128]{2,1,0:T(8,128)S(1)} %get-tuple-element.34), channel_id=1, source_target_pairs={{0,4},{4,0},{8,12},{12,8},{1,5},{5,1},{9,13},{13,9},{2,6},{6,2},{1... | collective-permute-start | bytes 393224 | tf_op jit(solution)/shard_map/ppermute | solution.py:251
  24.6 10.7 %collective-permute-start.17 = (f32[2,128,128]{2,1,0:T(8,128)S(1)}, f32[2,128,128]{2,1,0:T(8,128)S(1)}, u32[]{:S(2)}, u32[]{:S(2)}) collective-permute-start(f32[2,128,128]{2,1,0:T(8,128)S(1)} %get-tuple-element.28), channel_id=1, source_target_pairs={{0,1},{1,0},{2,3},{3,2},{4,5},{5,4},{6,7},{7,6},{8,9},{9,8},{10,11... | collective-permute-start | bytes 393224 | tf_op jit(solution)/shard_map/ppermute | solution.py:262
  24.7 7.7 %collective-permute-start.13 = (f32[2,128,128]{2,1,0:T(8,128)S(1)}, f32[2,128,128]{2,1,0:T(8,128)S(1)}, u32[]{:S(2)}, u32[]{:S(2)}) collective-permute-start(f32[2,128,128]{2,1,0:T(8,128)S(1)} %collective-permute-done.12), channel_id=1, source_target_pairs={{0,96},{96,0},{32,64},{64,32},{1,97},{97,1},{33,65},{65,33},{2,98}... | collective-permute-start | bytes 393224 | tf_op jit(solution)/shard_map/ppermute | solution.py:254
  26.6 11.8 %collective-permute-start.11 = (f32[2,2,128,128]{3,2,1,0:T(8,128)S(1)}, f32[2,2,128,128]{3,2,1,0:T(8,128)S(1)}, u32[]{:S(2)}, u32[]{:S(2)}) collective-permute-start(f32[2,2,128,128]{3,2,1,0:T(8,128)S(1)} %pad_maximum_fusion.2.b1), channel_id=1, source_target_pairs={{0,96},{96,0},{32,64},{64,32},{1,97},{97,1},{33,65},{65,33},{2,98}... | collective-permute-start | bytes 786440 | tf_op jit(solution)/shard_map/ppermute | solution.py:256
  28.8 6.3 %collective-permute-start.6 = (f32[2,128,128]{2,1,0:T(8,128)S(1)}, f32[2,128,128]{2,1,0:T(8,128)S(1)}, u32[]{:S(2)}, u32[]{:S(2)}) collective-permute-start(f32[2,128,128]{2,1,0:T(8,128)S(1)} %collective-permute-done.5), channel_id=1, source_target_pairs={{0,12},{12,0},{4,8},{8,4},{1,13},{13,1},{5,9},{9,5},{2,14},{14,2},... | collective-permute-start | bytes 393224 | tf_op jit(solution)/shard_map/ppermute | solution.py:253
  32.4 8.4 %collective-permute-start.4 = (f32[2,2,128,128]{3,2,1,0:T(8,128)S(1)}, f32[2,2,128,128]{3,2,1,0:T(8,128)S(1)}, u32[]{:S(2)}, u32[]{:S(2)}) collective-permute-start(f32[2,2,128,128]{3,2,1,0:T(8,128)S(1)} %pad_maximum_fusion.a1), channel_id=1, source_target_pairs={{0,12},{12,0},{4,8},{8,4},{1,13},{13,1},{5,9},{9,5},{2,14},{14,2},... | collective-permute-start | bytes 786440 | tf_op jit(solution)/shard_map/ppermute | solution.py:255
  35.2 7.0 %collective-permute-start.14 = (f32[2,2,128,128]{3,2,1,0:T(8,128)S(1)}, f32[2,2,128,128]{3,2,1,0:T(8,128)S(1)}, u32[]{:S(2)}, u32[]{:S(2)}) collective-permute-start(f32[2,2,128,128]{3,2,1,0:T(8,128)S(1)} %pad_maximum_fusion.3.b2), channel_id=1, source_target_pairs={{0,32},{32,0},{64,96},{96,64},{1,33},{33,1},{65,97},{97,65},{2,34}... | collective-permute-start | bytes 786440 | tf_op jit(solution)/shard_map/ppermute | solution.py:258
  35.3 7.0 %collective-permute-start.7 = (f32[2,2,128,128]{3,2,1,0:T(8,128)S(1)}, f32[2,2,128,128]{3,2,1,0:T(8,128)S(1)}, u32[]{:S(2)}, u32[]{:S(2)}) collective-permute-start(f32[2,2,128,128]{3,2,1,0:T(8,128)S(1)} %pad_maximum_fusion.1.a2), channel_id=1, source_target_pairs={{0,4},{4,0},{8,12},{12,8},{1,5},{5,1},{9,13},{13,9},{2,6},{6,2},{1... | collective-permute-start | bytes 786440 | tf_op jit(solution)/shard_map/ppermute | solution.py:257
  38.4 8.3 %collective-permute-start.18 = (f32[2,2,128,128]{3,2,1,0:T(8,128)S(1)}, f32[2,2,128,128]{3,2,1,0:T(8,128)S(1)}, u32[]{:S(2)}, u32[]{:S(2)}) collective-permute-start(f32[2,2,128,128]{3,2,1,0:T(8,128)S(1)} %pad_maximum_fusion.4), channel_id=1, source_target_pairs={{0,2},{2,0},{1,3},{3,1},{4,6},{6,4},{5,7},{7,5},{8,10},{10,8},{9,1... | collective-permute-start | bytes 786440 | tf_op jit(solution)/shard_map/ppermute | solution.py:263
  44.3 3.6 %collective-permute-start.15 = (f32[2,2,128,128]{3,2,1,0:T(8,128)S(1)}, f32[2,2,128,128]{3,2,1,0:T(8,128)S(1)}, u32[]{:S(2)}, u32[]{:S(2)}) collective-permute-start(f32[2,2,128,128]{3,2,1,0:T(8,128)S(1)} %get-tuple-element.14), channel_id=1, source_target_pairs={{0,1},{1,0},{2,3},{3,2},{4,5},{5,4},{6,7},{7,6},{8,9},{9,8},{10,11... | collective-permute-start | bytes 786440 | tf_op jit(solution)/shard_map/ppermute | solution.py:277
  49.1 12.1 %collective-permute-start.19 = (f32[128,128]{1,0:T(8,128)S(1)}, f32[128,128]{1,0:T(8,128)S(1)}, u32[]{:S(2)}, u32[]{:S(2)}) collective-permute-start(f32[128,128]{1,0:T(8,128)S(1)} %get-tuple-element.24), channel_id=1, source_target_pairs={{0,2},{2,0},{1,3},{3,1},{4,6},{6,4},{5,7},{7,5},{8,10},{10,8},{9,1... | collective-permute-start | bytes 196616 | tf_op jit(solution)/shard_map/ppermute | solution.py:285
  50.9 10.2 %collective-permute-start.20 = (f32[128,128]{1,0:T(8,128)S(1)}, f32[128,128]{1,0:T(8,128)S(1)}, u32[]{:S(2)}, u32[]{:S(2)}) collective-permute-start(f32[128,128]{1,0:T(8,128)S(1)} %get-tuple-element.26), channel_id=1, source_target_pairs={{0,16},{16,0},{1,17},{17,1},{2,18},{18,2},{3,19},{19,3},{4,20},{20... | collective-permute-start | bytes 196616 | tf_op jit(solution)/shard_map/ppermute | solution.py:286
  51.0 10.1 %collective-permute-start.21 = (f32[128,128]{1,0:T(8,128)S(1)}, f32[128,128]{1,0:T(8,128)S(1)}, u32[]{:S(2)}, u32[]{:S(2)}) collective-permute-start(f32[128,128]{1,0:T(8,128)S(1)} %get-tuple-element.25), channel_id=1, source_target_pairs={{0,18},{2,16},{16,2},{18,0},{1,19},{3,17},{17,3},{19,1},{4,22},{6,... | collective-permute-start | bytes 196616 | tf_op jit(solution)/shard_map/ppermute | solution.py:287
  53.2 19.8 %all-to-all-start = ((f32[64,16,128]{2,1,0:T(8,128)}), f32[64,16,128]{2,1,0:T(8,128)S(1)}, u32[]{:S(2)}, u32[]{:S(2)}) async-start(f32[64,16,128]{2,1,0:T(8,128)} %bitcast.23), calls=%async_computation | async-start | bytes 1048576 | tf_op jit(solution)/shard_map/all_to_all | solution.py:284
  (3 other events, 85.0 us)
where the time goes:
time: 73.9 us; the launch traced here: 73.7 us
  starting transfers between devices  47.2 us (64%)
  waiting for transfers between devices  18.1 us (24%)
  Pallas kernels  4.89 us (7%)
  other arithmetic  1.5 us (2%)
  local copies, waits for them, and re-layouts  1.06 us (1%)
  between operations  0.88 us (1%)
    all_to_all x1, waiting for transfers between devices, step(): lax.all_to_all(corr.reshape(64, 16, Q), ('x', 'zl', 'y', 'zh'), 0, 0, til...  11.1 us
    all_to_all x1, starting transfers between devices, step(): lax.all_to_all(corr.reshape(64, 16, Q), ('x', 'zl', 'y', 'zh'), 0, 0, til...  7.89 us
    ppermute x1, starting transfers between devices, step(): b34 = lax.ppermute(b12, 'y', ODD)  6.82 us
    pallas_call x4, Pallas kernels, call(): pl.pallas_call(body, out_shape=out_shape, in_specs=in_specs or [ALL_VMEM]...  4.89 us
    ppermute x1, starting transfers between devices, step(): a34 = lax.ppermute(a12, 'x', ODD)  2.84 us
    ppermute x1, starting transfers between devices, step(): a1r = lax.ppermute(a1, 'y', ODD)  2.74 us
    ppermute x1, starting transfers between devices, step(): a2 = jnp.stack([a34, lax.ppermute(a34, 'y', ODD)])  2.59 us
    ppermute x1, starting transfers between devices, step(): a2r = lax.ppermute(a2, 'y', EVEN)  2.4 us
  transfers between devices with their start and end apart: 23, of which 7 were waited for; matrix products, arithmetic and copies ran while one was open for 1% of the time, Pallas kernels for 5%

commit v1 on v0

v1 whole, which is shorter than its diff:
```python
import jax
import jax.numpy as jnp
import numpy as np
from jax import lax
from jax.experimental import pallas as pl
from jax.experimental.pallas import tpu as pltpu
from jax.sharding import Mesh, PartitionSpec as P


W = 512
BS = 64
Q = 128
AXES = ("x", "zl", "y", "zh", "core")
SIZES = (4, 2, 4, 2, 2)
PROW = ("x", "zl", "y")
PCOL = ("zh", "core")

SWAP = [(0, 1), (1, 0)]
EVEN = [(0, 1), (1, 0), (2, 3), (3, 2)]
FAR = [(0, 2), (2, 0), (1, 3), (3, 1)]
ODD = [(0, 3), (3, 0), (1, 2), (2, 1)]
ALL_VMEM = pl.BlockSpec(memory_space=pltpu.VMEM)


def route(where):
    pairs = []
    for source in np.ndindex(*SIZES):
        x, zl, y, zh, core = source
        target = where(x, zl, y, 2 * zh + core)
        tx, tzl, ty, tc = target
        pairs.append(
            (
                int(np.ravel_multi_index(source, SIZES)),
                int(np.ravel_multi_index((tx, tzl, ty, tc // 2, tc % 2), SIZES)),
            )
        )
    return pairs


def send(x, axes, pairs):
    return lax.ppermute(x, axes, pairs)


def pick(x, i, dim):
    return lax.dynamic_index_in_dim(x, i, dim, keepdims=False)


def split(v):
    high = v.astype(jnp.bfloat16)
    return high, (v - high.astype(jnp.float32)).astype(jnp.bfloat16)


def dot3(left, right):
    ah, al = left
    bh, bl = right

    def one(a, b):
        return jnp.dot(a, b, preferred_element_type=jnp.float32)

    return one(ah, bh) + (one(ah, bl) + one(al, bh))


def position():
    return [lax.axis_index(name) for name in AXES]


def call(body, out_shape, arrays, limit, in_specs=None, scratch=()):
    return pl.pallas_call(
        body,
        out_shape=out_shape,
        in_specs=in_specs or [ALL_VMEM] * len(arrays),
        out_specs=(ALL_VMEM,) * len(out_shape),
        scratch_shapes=scratch,
        compiler_params=pltpu.CompilerParams(vmem_limit_bytes=limit * 1024 * 1024),
    )(*arrays)


def early(
    counts_hbm,
    ancestors_hbm,
    diag_hbm,
    square,
    col_mask,
    row_mask,
    out_mask,
    diag_hi,
    diag_lo,
    tile,
    counts,
    ancestors,
    diag,
    sems,
):
    x, zl, y, zh, core = position()
    prow = 8 * x + 4 * zl + y
    pcol = 2 * zh + core
    fetch = [
        pltpu.make_async_copy(counts_hbm, counts, sems.at[0]),
        pltpu.make_async_copy(ancestors_hbm, ancestors, sems.at[1]),
        pltpu.make_async_copy(diag_hbm, diag, sems.at[2]),
    ]
    for copy in fetch:
        copy.start()
    for copy in fetch[:2]:
        copy.wait()
    lane = lax.broadcasted_iota(jnp.int32, (32, 63), 1)
    slot = lax.broadcasted_iota(jnp.int32, (32, 63), 0)
    row_group = jnp.where(slot < 18, prow, prow + 4 - 8 * zl)
    block = jnp.where(slot < 16, (slot // 2) * 4 + pcol, row_group) + (slot % 2) * 32
    found = []
    for s in range(2):
        hit = (ancestors[s : s + 1, :] == block) & (lane < counts[s])
        found.append(jnp.max(hit.astype(jnp.float32), axis=1, keepdims=True))
        for j in range(2):
            out_mask[s, j * BS : (j + 1) * BS, :] = jnp.broadcast_to(found[s][16 + j : 17 + j, :], (BS, Q))
    owned = jnp.where(zl == 0, found[0], found[1])
    column = lax.broadcasted_iota(jnp.int32, (1, 8 * Q), 1) // BS
    mask = jnp.zeros((1, 8 * Q), jnp.float32)
    for j in range(16):
        mask = jnp.where(column == j, owned[j : j + 1, :], mask)
    col_mask[...] = mask
    for j in range(4):
        row_mask[j * BS : (j + 1) * BS, :] = jnp.broadcast_to(owned[16 + j : 17 + j, :], (BS, Q))
    fetch[2].wait()
    for s in range(2):
        left = diag[s, :, pl.ds(pl.multiple_of((prow // 8) * Q, Q), Q)]
        right = diag[s, :, pl.ds(pl.multiple_of(pcol * Q, Q), Q)]
        tile[...] = dot3(split(left.T), split(right))
        square[s] = tile[pl.ds(pl.multiple_of((prow % 8) * 16, 16), 16), :]
    hi, lo = split(diag[zl])
    diag_hi[...] = hi
    diag_lo[...] = lo


def left_factor(diag_hi, diag_lo, row_mask, mine, g_zl, g_core, g_zh, hi_t, lo_t):
    _, _, _, zh, core = position()
    pcol = 2 * zh + core
    quarters = (
        (mine[...], g_zl[...], pcol),
        (g_core[0], g_core[1], 2 * zh + 1 - core),
        (g_zh[0, 0], g_zh[0, 1], 2 - 2 * zh + core),
        (g_zh[1, 0], g_zh[1, 1], 3 - 2 * zh - core),
    )
    scaled = jnp.zeros((2 * Q, W), jnp.float32)
    for own, partner, quarter in quarters:
        rows = jnp.concatenate([own, partner], axis=0) * row_mask[...]
        start = pl.multiple_of(quarter * Q, Q)
        scaled = scaled + dot3(split(rows), (diag_hi[pl.ds(start, Q), :], diag_lo[pl.ds(start, Q), :]))
    hi, lo = split(scaled.T)
    hi_t[...] = hi
    lo_t[...] = lo


def products(
    band_own,
    band_other,
    col_mask,
    a_all,
    a_even,
    a_far,
    a_odd,
    b_all,
    b_even,
    b_far,
    b_odd,
    diag_hi,
    diag_lo,
    part_keep,
    part_send,
    band_hi,
    band_lo,
    panel_hi,
    panel_lo,
    turned_hi,
    turned_lo,
):
    x, zl, y, zh, core = position()
    pieces = {}
    for outer, refs in enumerate(((a_all, a_even, a_far, a_odd), (b_all, b_even, b_far, b_odd))):
        for far, ref in enumerate(refs):
            for near in range(4):
                xo, q = (near, far) if outer == 0 else (far, near)
                pieces[outer, xo, q] = ref.at[near]
    for (stream, xo, q), ref in pieces.items():
        hi, lo = split(ref[...])
        rows = slice((2 * xo + stream) * Q, (2 * xo + stream + 1) * Q)
        cols = slice(q * Q, (q + 1) * Q)
        panel_hi[rows, cols] = hi
        panel_lo[rows, cols] = lo
    for xo in range(4):
        for stream in range(2):
            side = zl if stream == 0 else 1 - zl
            start = pl.multiple_of((x ^ xo) * (2 * Q) + side * Q, Q)
            mask = col_mask[:, pl.ds(start, Q)]
            cols = slice((2 * xo + stream) * Q, (2 * xo + stream + 1) * Q)
            for r, ref in enumerate((band_own, band_other)):
                hi, lo = split(ref[:, pl.ds(start, Q)] * mask)
                band_hi[r * Q : (r + 1) * Q, cols] = hi
                band_lo[r * Q : (r + 1) * Q, cols] = lo
    for q in range(4):
        start = pl.multiple_of((y ^ q) * Q, Q)
        turned_hi[q * Q : (q + 1) * Q, :] = diag_hi[pl.ds(start, Q), :]
        turned_lo[q * Q : (q + 1) * Q, :] = diag_lo[pl.ds(start, Q), :]
    product = dot3((band_hi[...], band_lo[...]), (panel_hi[...], panel_lo[...]))
    partial = dot3(split(product), (turned_hi[...], turned_lo[...]))
    for c in range(2):

        @pl.when(core == c)
        def _():
            for h in range(2):
                side = jnp.where(zh == h, 0, 1)
                for ref, k in ((part_keep, c), (part_send, 1 - c)):
                    part = partial[:, (2 * h + k) * Q : (2 * h + k + 1) * Q]
                    ref[:, side] = part.reshape(2, Q, Q)


def correction(part_keep, part_got, left_hi, left_lo, part, corr):
    _, _, _, zh, _ = position()
    part[...] = part_keep[...] + part_got[...]
    right = jnp.concatenate(
        [jnp.concatenate([part[0, s], part[1, s]], axis=0) for s in range(2)], axis=1
    )
    value = dot3((left_hi[...], left_lo[...]), split(right))
    corr[:, zh] = value[:, :Q].reshape(32, 16, Q)
    corr[:, 1 - zh] = value[:, Q:].reshape(32, 16, Q)


def finish(part, in_a, in_b, in_c, out_mask, landed, square, new_column, diag_block):
    _, zl, _, _, _ = position()
    new_column[zl] = -((part[...] + in_a[...]) * out_mask[zl])
    new_column[1 - zl] = -((in_b[...] + in_c[...]) * out_mask[1 - zl])
    for s in range(2):
        total = square[s]
        for i in range(4):
            for j in range(8):
                total = total + landed[i, s, j]
        diag_block[s] = total


def f32(*shape):
    return jax.ShapeDtypeStruct(shape, jnp.float32)


def bf16(*shape):
    return jax.ShapeDtypeStruct(shape, jnp.bfloat16)


def vmem(*shapes):
    return [pltpu.VMEM(shape, jnp.bfloat16) for shape in shapes]


def step(band, panel, diag_inverse, ancestors, counts):
    zl = lax.axis_index("zl")
    mine = pick(panel, zl, 0)
    other = pick(panel, 1 - zl, 0)
    a_here = send(mine, AXES, route(lambda x, zl, y, c: (x, zl, c, y)))
    b_here = send(other, AXES, route(lambda x, zl, y, c: (x, 1 - zl, c, y)))
    band_other = send(band, "zl", SWAP)

    square, col_mask, row_mask, out_mask, diag_hi, diag_lo = call(
        early,
        (f32(2, 16, Q), f32(1, 8 * Q), f32(2 * Q, Q), f32(2, Q, Q), bf16(W, W), bf16(W, W)),
        [pltpu.with_memory_space_constraint(v, pltpu.HBM) for v in (counts, ancestors, diag_inverse)],
        12,
        in_specs=[pl.BlockSpec(memory_space=pltpu.HBM)] * 3,
        scratch=[
            pltpu.VMEM((Q, Q), jnp.float32),
            pltpu.SMEM((2,), jnp.int32),
            pltpu.VMEM((2, 63), jnp.int32),
            pltpu.VMEM((2, W, W), jnp.float32),
            pltpu.SemaphoreType.DMA((3,)),
        ],
    )
    a4 = jnp.stack(
        [a_here, send(a_here, "x", EVEN), send(a_here, "x", FAR), send(a_here, "x", ODD)]
    )
    b4 = jnp.stack(
        [b_here, send(b_here, "y", EVEN), send(b_here, "y", FAR), send(b_here, "y", ODD)]
    )
    a_even, b_even = send(a4, "y", EVEN), send(b4, "x", EVEN)
    a_far, b_far = send(a4, "y", FAR), send(b4, "x", FAR)
    a_odd, b_odd = send(a4, "y", ODD), send(b4, "x", ODD)

    g_zl = send(other, "zl", SWAP)
    rows = jnp.stack([mine, g_zl])
    g_core = send(rows, "core", SWAP)
    g_zh = send(jnp.stack([rows, g_core]), "zh", SWAP)
    left_hi, left_lo = call(
        left_factor,
        (bf16(W, 2 * Q), bf16(W, 2 * Q)),
        (diag_hi, diag_lo, row_mask, mine, g_zl, g_core, g_zh),
        12,
    )
    part_keep, part_send = call(
        products,
        (f32(2, 2, Q, Q), f32(2, 2, Q, Q)),
        (
            (band, band_other, col_mask)
            + (a4, a_even, a_far, a_odd)
            + (b4, b_even, b_far, b_odd)
            + (diag_hi, diag_lo)
        ),
        20,
        scratch=vmem(*[(2 * Q, 8 * Q)] * 2, *[(8 * Q, W)] * 2, *[(W, W)] * 2),
    )
    part_got = send(part_send, "core", SWAP)
    parts, corr = call(
        correction,
        (f32(2, 2, Q, Q), f32(32, 2, 16, Q)),
        (part_keep, part_got, left_hi, left_lo),
        12,
    )
    landed = lax.all_to_all(corr.reshape(64, 16, Q), ("x", "zl", "y", "zh"), 0, 0, tiled=True)
    in_a = send(parts[0, 1], "zh", SWAP)
    in_b = send(parts[1, 0], "zl", SWAP)
    in_c = send(parts[1, 1], ("zl", "zh"), [(0, 3), (1, 2), (2, 1), (3, 0)])
    return call(
        finish,
        (f32(2, Q, Q), f32(2, 16, Q)),
        (parts[0, 0], in_a, in_b, in_c, out_mask, landed.reshape(4, 2, 8, 16, Q), square),
        12,
    )


def solution(mesh):
    fine = Mesh(mesh.devices.reshape(SIZES), AXES)
    in_specs = (P(PROW, PCOL), P(None, PROW, PCOL), P(), P(), P())
    out_specs = (P(None, PROW, PCOL), P(None, PROW, PCOL))
    return jax.shard_map(step, mesh=fine, in_specs=in_specs, out_specs=out_specs, check_vma=False)
```

time: 73.9 us -> 83.5 us (1.13)
  waiting for transfers between devices: 18.1 us -> 27.6 us
  Pallas kernels: 4.89 us -> 7.24 us
  other arithmetic: 1.5 us -> 0.08 us
    ppermute x22, waiting for transfers between devices: 6.97 us -> 25.8 us  [send(): return lax.ppermute(x, axes, pairs)]
    all_to_all x1, waiting for transfers between devices: 11.1 us -> 1.75 us  [step(): lax.all_to_all(corr.reshape(64, 16, Q), ('x', 'zl', 'y', 'zh'), 0, 0, til...]
    pallas_call x4 -> x5, Pallas kernels: 4.89 us -> 7.24 us  [call(): pl.pallas_call(body, out_shape=out_shape, in_specs=in_specs or [ALL_VMEM]...]
  transfers between devices with their start and end apart: 23 -> 23, of which waited for: 7 -> 9; matrix products, arithmetic and copies ran while one was open for 1% -> 0% of each run, Pallas kernels for 5% -> 6%
where the time goes in v1:
time: 83.5 us; the launch traced here: 83.2 us
  starting transfers between devices  46.6 us (56%)
  waiting for transfers between devices  27.6 us (33%)
  Pallas kernels  7.24 us (9%)
  local copies, waits for them, and re-layouts  0.91 us (1%)
    ppermute x22, starting transfers between devices, send(): return lax.ppermute(x, axes, pairs)  39 us
    ppermute x22, waiting for transfers between devices, send(): return lax.ppermute(x, axes, pairs)  25.8 us
    all_to_all x1, starting transfers between devices, step(): lax.all_to_all(corr.reshape(64, 16, Q), ('x', 'zl', 'y', 'zh'), 0, 0, til...  7.66 us
    pallas_call x5, Pallas kernels, call(): pl.pallas_call(body, out_shape=out_shape, in_specs=in_specs or [ALL_VMEM]...  7.24 us
    all_to_all x1, waiting for transfers between devices, step(): lax.all_to_all(corr.reshape(64, 16, Q), ('x', 'zl', 'y', 'zh'), 0, 0, til...  1.75 us
  transfers between devices with their start and end apart: 23, of which 9 were waited for; matrix products, arithmetic and copies ran while one was open for 0% of the time, Pallas kernels for 6%

profile of v1, /device:TPU:0, one launch (start us, length us, event | category | flops | bytes accessed | tf_op | source)
XLA Modules:
  0.0 83.2 jit_solution(9322512788306923154)
XLA Ops:
  0.6 0.9 %dynamic-slice_bitcast_fusion = (f32[128,128]{1,0:T(8,128)S(1)}, f32[1,128,128]{2,1,0:T(8,128)S(1)}) fusion(f32[2,128,128]{2,1,0:T(8,128)} %param.6, s32[]{:T(128)S(6)} %select_n.8, s32[]{:T(128)S(6)} %select_n.7), kind=kLoop, calls=%fused_computation.8 | loop fusion | bytes 262152 | tf_op jit(solution)/shard_map/jit(dynamic_index_in_dim)/squeeze | solution.py:45
  2.3 2.1 %collective-permute-start.8 = (f32[128,128]{1,0:T(8,128)S(1)}, f32[128,128]{1,0:T(8,128)S(1)}, u32[]{:S(2)}, u32[]{:S(2)}) collective-permute-start(f32[128,128]{1,0:T(8,128)S(1)} %get-tuple-element.32), channel_id=1, source_target_pairs={{0,16},{1,20},{2,24},{3,28},{4,17},{5,21},{6,25},{7,29},{8,18},{9,... | collective-permute-start | bytes 196616 | tf_op jit(solution)/shard_map/ppermute | solution.py:41
  4.5 2.8 %collective-permute-start.4 = (f32[128,128]{1,0:T(8,128)S(1)}, f32[128,128]{1,0:T(8,128)S(1)}, u32[]{:S(2)}, u32[]{:S(2)}) collective-permute-start(f32[128,128]{1,0:T(8,128)S(1)} %collective-permute-done.1), channel_id=1, source_target_pairs={{0,96},{96,0},{32,64},{64,32},{1,97},{97,1},{33,65},{65,33},{2,98}... | collective-permute-start | bytes 196616 | tf_op jit(solution)/shard_map/ppermute | solution.py:41
  7.2 0.8 collective-permute-start.3
  8.7 13.0 %collective-permute-start.11 = (f32[128,128]{1,0:T(8,128)S(1)}, f32[128,128]{1,0:T(8,128)S(1)}, u32[]{:S(2)}, u32[]{:S(2)}) collective-permute-start(f32[128,128]{1,0:T(8,128)S(1)} %collective-permute-done.8), channel_id=1, source_target_pairs={{0,12},{12,0},{4,8},{8,4},{1,13},{13,1},{5,9},{9,5},{2,14},{14,2},... | collective-permute-start | bytes 196616 | tf_op jit(solution)/shard_map/ppermute | solution.py:41
  21.7 2.9 %collective-permute-start.6 = (f32[4,128,128]{2,1,0:T(8,128)S(1)}, f32[4,128,128]{2,1,0:T(8,128)S(1)}, u32[]{:S(2)}, u32[]{:S(2)}) collective-permute-start(f32[4,128,128]{2,1,0:T(8,128)S(1)} %pad_maximum_fusion.a_all), channel_id=1, source_target_pairs={{0,8},{8,0},{4,12},{12,4},{1,9},{9,1},{5,13},{13,5},{2,10},{10,2},... | collective-permute-start | bytes 786440 | tf_op jit(solution)/shard_map/ppermute | solution.py:41
  24.6 3.0 %collective-permute-start = (f32[128,1024]{1,0:T(8,128)}, f32[128,1024]{1,0:T(8,128)S(1)}, u32[]{:S(2)}, u32[]{:S(2)}) collective-permute-start(f32[128,1024]{1,0:T(8,128)} %band_own.1), channel_id=1, source_target_pairs={{0,16},{16,0},{1,17},{17,1},{2,18},{18,2},{3,19},{19,3},{4,20},{20... | collective-permute-start | bytes 1572872 | tf_op jit(solution)/shard_map/ppermute | solution.py:41
  27.7 8.4 %collective-permute-done.10 = f32[128,128]{1,0:T(8,128)S(1)} collective-permute-done((f32[128,128]{1,0:T(8,128)S(1)}, f32[128,128]{1,0:T(8,128)S(1)}, u32[]{:S(2)}, u32[]{:S(2)}) %collective-permute-start.10) | collective-permute-done | bytes 65568 | tf_op jit(solution)/shard_map/ppermute | solution.py:41
  36.2 1.3 %collective-permute-start.7 = (f32[4,128,128]{2,1,0:T(8,128)S(1)}, f32[4,128,128]{2,1,0:T(8,128)S(1)}, u32[]{:S(2)}, u32[]{:S(2)}) collective-permute-start(f32[4,128,128]{2,1,0:T(8,128)S(1)} %pad_maximum_fusion.a_all), channel_id=1, source_target_pairs={{0,12},{12,0},{4,8},{8,4},{1,13},{13,1},{5,9},{9,5},{2,14},{14,2},... | collective-permute-start | bytes 786440 | tf_op jit(solution)/shard_map/ppermute | solution.py:41
  37.5 1.6 %collective-permute-start.12 = (f32[4,128,128]{2,1,0:T(8,128)S(1)}, f32[4,128,128]{2,1,0:T(8,128)S(1)}, u32[]{:S(2)}, u32[]{:S(2)}) collective-permute-start(f32[4,128,128]{2,1,0:T(8,128)S(1)} %pad_maximum_fusion.1.b_all), channel_id=1, source_target_pairs={{0,32},{32,0},{64,96},{96,64},{1,33},{33,1},{65,97},{97,65},{2,34}... | collective-permute-start | bytes 786440 | tf_op jit(solution)/shard_map/ppermute | solution.py:41
  39.1 2.7 %collective-permute-start.13 = (f32[4,128,128]{2,1,0:T(8,128)S(1)}, f32[4,128,128]{2,1,0:T(8,128)S(1)}, u32[]{:S(2)}, u32[]{:S(2)}) collective-permute-start(f32[4,128,128]{2,1,0:T(8,128)S(1)} %pad_maximum_fusion.1.b_all), channel_id=1, source_target_pairs={{0,64},{64,0},{32,96},{96,32},{1,65},{65,1},{33,97},{97,33},{2,66}... | collective-permute-start | bytes 786440 | tf_op jit(solution)/shard_map/ppermute | solution.py:41
  42.3 2.3 %shard_map.68 = (f32[2,16,128]{2,1,0:T(8,128)S(1)}, f32[1,1024]{1,0:T(1,128)S(1)}, f32[256,128]{1,0:T(8,128)S(1)}, f32[2,128,128]{2,1,0:T(8,128)S(1)}, bf16[512,...) custom-call(s32[2]{0:T(128)} %counts_hbm.1, s32[2,63]{1,0:T(2,128)} %ancestors_hbm.1, f32[2,512,512]{2,1,0:T(8,128)} %diag_hbm.1), custom_call_target="tpu_custom_call" | custom-call | tf_op jit(solution)/shard_map/pallas_call | solution.py:68
  44.7 1.4 %collective-permute-done.7.a_odd = f32[4,128,128]{2,1,0:T(8,128)S(1)} collective-permute-done((f32[4,128,128]{2,1,0:T(8,128)S(1)}, f32[4,128,128]{2,1,0:T(8,128)S(1)}, u32[]{:S(2)}, u32[]{:S(2)}) %collective-permute-start.7) | collective-permute-done | bytes 262176 | tf_op jit(solution)/shard_map/ppermute | solution.py:41
  46.1 2.4 %collective-permute-start.18 = (f32[2,2,128,128]{3,2,1,0:T(8,128)S(1)}, f32[2,2,128,128]{3,2,1,0:T(8,128)S(1)}, u32[]{:S(2)}, u32[]{:S(2)}) collective-permute-start(f32[2,2,128,128]{3,2,1,0:T(8,128)S(1)} %pad_maximum_fusion.2), channel_id=1, source_target_pairs={{0,2},{2,0},{1,3},{3,1},{4,6},{6,4},{5,7},{7,5},{8,10},{10,8},{9,1... | collective-permute-start | bytes 786440 | tf_op jit(solution)/shard_map/ppermute | solution.py:41
  48.5 5.5 %collective-permute-done.13.b_far = f32[4,128,128]{2,1,0:T(8,128)S(1)} collective-permute-done((f32[4,128,128]{2,1,0:T(8,128)S(1)}, f32[4,128,128]{2,1,0:T(8,128)S(1)}, u32[]{:S(2)}, u32[]{:S(2)}) %collective-permute-start.13) | collective-permute-done | bytes 262176 | tf_op jit(solution)/shard_map/ppermute | solution.py:41
  54.0 2.6 %collective-permute-done.14.b_odd = f32[4,128,128]{2,1,0:T(8,128)S(1)} collective-permute-done((f32[4,128,128]{2,1,0:T(8,128)S(1)}, f32[4,128,128]{2,1,0:T(8,128)S(1)}, u32[]{:S(2)}, u32[]{:S(2)}) %collective-permute-start.14) | collective-permute-done | bytes 262176 | tf_op jit(solution)/shard_map/ppermute | solution.py:41
  56.5 1.9 %shard_map.69 = (f32[2,2,128,128]{3,2,1,0:T(8,128)S(1)}, f32[2,2,128,128]{3,2,1,0:T(8,128)S(1)}) custom-call(f32[128,1024]{1,0:T(8,128)S(1)} %copy-done, f32[128,1024]{1,0:T(8,128)S(1)} %collective-permute-done.band_other, f32[1,1024]{1,0:T(1,128)S(1)} %get-tuple-element.14.col_mask, f32[4,128,128]{2,1,0:T(8,128)S(1)} %pad_maximum_fusion.a_all, ...), custom_call_target="tpu_custom_call" | custom-call | tf_op jit(solution)/shard_map/pallas_call | solution.py:68
  58.6 1.1 %shard_map.70 = (bf16[512,256]{1,0:T(8,128)(2,1)S(1)}, bf16[512,256]{1,0:T(8,128)(2,1)S(1)}) custom-call(bf16[512,512]{1,0:T(8,128)(2,1)S(1)} %get-tuple-element.15.diag_hi, bf16[512,512]{1,0:T(8,128)(2,1)S(1)} %get-tuple-element.16.diag_lo, f32[256,128]{1,0:T(8,128)S(1)} %get-tuple-element.19.row_mask, f32[128,128]{1,0:T(8,128)S(1)} %bitcast.27, ...), custom_call_target="tpu_custom_call" | custom-call | tf_op jit(solution)/shard_map/pallas_call | solution.py:68
  60.1 1.2 %shard_map.71 = (f32[2,2,128,128]{3,2,1,0:T(8,128)S(1)}, f32[32,2,16,128]{3,2,1,0:T(8,128)}) custom-call(f32[2,2,128,128]{3,2,1,0:T(8,128)S(1)} %get-tuple-element.17.part_keep, f32[2,2,128,128]{3,2,1,0:T(8,128)S(1)} %collective-permute-done.15.part_got, bf16[512,256]{1,0:T(8,128)(2,1)S(1)} %get-tuple-element.20.left_hi, ...), custom_call_target="tpu_custom_call" | custom-call | tf_op jit(solution)/shard_map/pallas_call | solution.py:68
  61.3 7.7 %all-to-all-start = ((f32[64,16,128]{2,1,0:T(8,128)}), f32[64,16,128]{2,1,0:T(8,128)S(1)}, u32[]{:S(2)}, u32[]{:S(2)}) async-start(f32[64,16,128]{2,1,0:T(8,128)} %bitcast.17), calls=%async_computation | async-start | bytes 1048576 | tf_op jit(solution)/shard_map/all_to_all | solution.py:313
  69.0 3.2 %collective-permute-start.19 = (f32[128,128]{1,0:T(8,128)S(1)}, f32[128,128]{1,0:T(8,128)S(1)}, u32[]{:S(2)}, u32[]{:S(2)}) collective-permute-start(f32[128,128]{1,0:T(8,128)S(1)} %get-tuple-element.28), channel_id=1, source_target_pairs={{0,2},{2,0},{1,3},{3,1},{4,6},{6,4},{5,7},{7,5},{8,10},{10,8},{9,1... | collective-permute-start | bytes 196616 | tf_op jit(solution)/shard_map/ppermute | solution.py:41
  73.3 4.5 %collective-permute-done.19.in_a = f32[128,128]{1,0:T(8,128)S(1)} collective-permute-done((f32[128,128]{1,0:T(8,128)S(1)}, f32[128,128]{1,0:T(8,128)S(1)}, u32[]{:S(2)}, u32[]{:S(2)}) %collective-permute-start.19) | collective-permute-done | bytes 65568 | tf_op jit(solution)/shard_map/ppermute | solution.py:41
  77.8 2.7 %collective-permute-done.20.in_b = f32[128,128]{1,0:T(8,128)S(1)} collective-permute-done((f32[128,128]{1,0:T(8,128)S(1)}, f32[128,128]{1,0:T(8,128)S(1)}, u32[]{:S(2)}, u32[]{:S(2)}) %collective-permute-start.20) | collective-permute-done | bytes 65568 | tf_op jit(solution)/shard_map/ppermute | solution.py:41
  80.8 1.7 %all-to-all-done = f32[64,16,128]{2,1,0:T(8,128)S(1)} async-done(((f32[64,16,128]{2,1,0:T(8,128)}), f32[64,16,128]{2,1,0:T(8,128)S(1)}, u32[]{:S(2)}, u32[]{:S(2)}) %all-to-all-start) | async-done | bytes 524320 | tf_op jit(solution)/shard_map/all_to_all | solution.py:313
  (35 shorter events, 4.9 us)
Async XLA Ops:
  1.5 55.0 %copy-start = (f32[128,1024]{1,0:T(8,128)S(1)}, f32[128,1024]{1,0:T(8,128)}, u32[]{:S(2)}) copy-start(f32[128,1024]{1,0:T(8,128)} %band_own.1) | copy-start | bytes 1572868
  1.5 2.9 %collective-permute-start.1 = (f32[128,128]{1,0:T(8,128)S(1)}, f32[128,128]{1,0:T(8,128)S(1)}, u32[]{:S(2)}, u32[]{:S(2)}) collective-permute-start(f32[128,128]{1,0:T(8,128)S(1)} %bitcast.26), channel_id=1, source_target_pairs={{0,0},{1,4},{2,8},{3,12},{4,1},{5,5},{6,9},{7,13},{8,2},{9,6},{10,... | collective-permute-start | bytes 196616 | tf_op jit(solution)/shard_map/ppermute | solution.py:41
  2.3 6.3 %collective-permute-start.8 = (f32[128,128]{1,0:T(8,128)S(1)}, f32[128,128]{1,0:T(8,128)S(1)}, u32[]{:S(2)}, u32[]{:S(2)}) collective-permute-start(f32[128,128]{1,0:T(8,128)S(1)} %get-tuple-element.32), channel_id=1, source_target_pairs={{0,16},{1,20},{2,24},{3,28},{4,17},{5,21},{6,25},{7,29},{8,18},{9,... | collective-permute-start | bytes 196616 | tf_op jit(solution)/shard_map/ppermute | solution.py:41
  4.5 17.2 %collective-permute-start.4 = (f32[128,128]{1,0:T(8,128)S(1)}, f32[128,128]{1,0:T(8,128)S(1)}, u32[]{:S(2)}, u32[]{:S(2)}) collective-permute-start(f32[128,128]{1,0:T(8,128)S(1)} %collective-permute-done.1), channel_id=1, source_target_pairs={{0,96},{96,0},{32,64},{64,32},{1,97},{97,1},{33,65},{65,33},{2,98}... | collective-permute-start | bytes 196616 | tf_op jit(solution)/shard_map/ppermute | solution.py:41
  7.2 14.4 %collective-permute-start.3 = (f32[128,128]{1,0:T(8,128)S(1)}, f32[128,128]{1,0:T(8,128)S(1)}, u32[]{:S(2)}, u32[]{:S(2)}) collective-permute-start(f32[128,128]{1,0:T(8,128)S(1)} %collective-permute-done.1), channel_id=1, source_target_pairs={{0,64},{64,0},{32,96},{96,32},{1,65},{65,1},{33,97},{97,33},{2,66}... | collective-permute-start | bytes 196616 | tf_op jit(solution)/shard_map/ppermute | solution.py:41
  8.0 13.6 %collective-permute-start.2 = (f32[128,128]{1,0:T(8,128)S(1)}, f32[128,128]{1,0:T(8,128)S(1)}, u32[]{:S(2)}, u32[]{:S(2)}) collective-permute-start(f32[128,128]{1,0:T(8,128)S(1)} %collective-permute-done.1), channel_id=1, source_target_pairs={{0,32},{32,0},{64,96},{96,64},{1,33},{33,1},{65,97},{97,65},{2,34}... | collective-permute-start | bytes 196616 | tf_op jit(solution)/shard_map/ppermute | solution.py:41
  8.5 19.1 %collective-permute-start.16 = (f32[128,128]{1,0:T(8,128)S(1)}, f32[128,128]{1,0:T(8,128)S(1)}, u32[]{:S(2)}, u32[]{:S(2)}) collective-permute-start(f32[128,128]{1,0:T(8,128)S(1)} %get-tuple-element.32), channel_id=1, source_target_pairs={{0,16},{16,0},{1,17},{17,1},{2,18},{18,2},{3,19},{19,3},{4,20},{20... | collective-permute-start | bytes 196616 | tf_op jit(solution)/shard_map/ppermute | solution.py:41
  8.7 19.0 %collective-permute-start.11 = (f32[128,128]{1,0:T(8,128)S(1)}, f32[128,128]{1,0:T(8,128)S(1)}, u32[]{:S(2)}, u32[]{:S(2)}) collective-permute-start(f32[128,128]{1,0:T(8,128)S(1)} %collective-permute-done.8), channel_id=1, source_target_pairs={{0,12},{12,0},{4,8},{8,4},{1,13},{13,1},{5,9},{9,5},{2,14},{14,2},... | collective-permute-start | bytes 196616 | tf_op jit(solution)/shard_map/ppermute | solution.py:41
  21.7 17.4 %collective-permute-start.5 = (f32[4,128,128]{2,1,0:T(8,128)S(1)}, f32[4,128,128]{2,1,0:T(8,128)S(1)}, u32[]{:S(2)}, u32[]{:S(2)}) collective-permute-start(f32[4,128,128]{2,1,0:T(8,128)S(1)} %pad_maximum_fusion.a_all), channel_id=1, source_target_pairs={{0,4},{4,0},{8,12},{12,8},{1,5},{5,1},{9,13},{13,9},{2,6},{6,2},{1... | collective-permute-start | bytes 786440 | tf_op jit(solution)/shard_map/ppermute | solution.py:41
  21.7 20.1 %collective-permute-start.6 = (f32[4,128,128]{2,1,0:T(8,128)S(1)}, f32[4,128,128]{2,1,0:T(8,128)S(1)}, u32[]{:S(2)}, u32[]{:S(2)}) collective-permute-start(f32[4,128,128]{2,1,0:T(8,128)S(1)} %pad_maximum_fusion.a_all), channel_id=1, source_target_pairs={{0,8},{8,0},{4,12},{12,4},{1,9},{9,1},{5,13},{13,5},{2,10},{10,2},... | collective-permute-start | bytes 786440 | tf_op jit(solution)/shard_map/ppermute | solution.py:41
  24.6 31.9 %collective-permute-start = (f32[128,1024]{1,0:T(8,128)}, f32[128,1024]{1,0:T(8,128)S(1)}, u32[]{:S(2)}, u32[]{:S(2)}) collective-permute-start(f32[128,1024]{1,0:T(8,128)} %band_own.1), channel_id=1, source_target_pairs={{0,16},{16,0},{1,17},{17,1},{2,18},{18,2},{3,19},{19,3},{4,20},{20... | collective-permute-start | bytes 1572872 | tf_op jit(solution)/shard_map/ppermute | solution.py:41
  27.6 8.6 %collective-permute-start.10 = (f32[128,128]{1,0:T(8,128)S(1)}, f32[128,128]{1,0:T(8,128)S(1)}, u32[]{:S(2)}, u32[]{:S(2)}) collective-permute-start(f32[128,128]{1,0:T(8,128)S(1)} %collective-permute-done.8), channel_id=1, source_target_pairs={{0,8},{8,0},{4,12},{12,4},{1,9},{9,1},{5,13},{13,5},{2,10},{10,2},... | collective-permute-start | bytes 196616 | tf_op jit(solution)/shard_map/ppermute | solution.py:41
  27.6 8.5 %collective-permute-start.9 = (f32[128,128]{1,0:T(8,128)S(1)}, f32[128,128]{1,0:T(8,128)S(1)}, u32[]{:S(2)}, u32[]{:S(2)}) collective-permute-start(f32[128,128]{1,0:T(8,128)S(1)} %collective-permute-done.8), channel_id=1, source_target_pairs={{0,4},{4,0},{8,12},{12,8},{1,5},{5,1},{9,13},{13,9},{2,6},{6,2},{1... | collective-permute-start | bytes 196616 | tf_op jit(solution)/shard_map/ppermute | solution.py:41
  36.2 1.3 %collective-permute-start.17 = (f32[2,128,128]{2,1,0:T(8,128)S(1)}, f32[2,128,128]{2,1,0:T(8,128)S(1)}, u32[]{:S(2)}, u32[]{:S(2)}) collective-permute-start(f32[2,128,128]{2,1,0:T(8,128)S(1)} %get-tuple-element.31), channel_id=1, source_target_pairs={{0,1},{1,0},{2,3},{3,2},{4,5},{5,4},{6,7},{7,6},{8,9},{9,8},{10,11... | collective-permute-start | bytes 393224 | tf_op jit(solution)/shard_map/ppermute | solution.py:41
  36.2 9.9 %collective-permute-start.7 = (f32[4,128,128]{2,1,0:T(8,128)S(1)}, f32[4,128,128]{2,1,0:T(8,128)S(1)}, u32[]{:S(2)}, u32[]{:S(2)}) collective-permute-start(f32[4,128,128]{2,1,0:T(8,128)S(1)} %pad_maximum_fusion.a_all), channel_id=1, source_target_pairs={{0,12},{12,0},{4,8},{8,4},{1,13},{13,1},{5,9},{9,5},{2,14},{14,2},... | collective-permute-start | bytes 786440 | tf_op jit(solution)/shard_map/ppermute | solution.py:41
  37.5 10.9 %collective-permute-start.12 = (f32[4,128,128]{2,1,0:T(8,128)S(1)}, f32[4,128,128]{2,1,0:T(8,128)S(1)}, u32[]{:S(2)}, u32[]{:S(2)}) collective-permute-start(f32[4,128,128]{2,1,0:T(8,128)S(1)} %pad_maximum_fusion.1.b_all), channel_id=1, source_target_pairs={{0,32},{32,0},{64,96},{96,64},{1,33},{33,1},{65,97},{97,65},{2,34}... | collective-permute-start | bytes 786440 | tf_op jit(solution)/shard_map/ppermute | solution.py:41
  39.1 14.9 %collective-permute-start.13 = (f32[4,128,128]{2,1,0:T(8,128)S(1)}, f32[4,128,128]{2,1,0:T(8,128)S(1)}, u32[]{:S(2)}, u32[]{:S(2)}) collective-permute-start(f32[4,128,128]{2,1,0:T(8,128)S(1)} %pad_maximum_fusion.1.b_all), channel_id=1, source_target_pairs={{0,64},{64,0},{32,96},{96,32},{1,65},{65,1},{33,97},{97,33},{2,66}... | collective-permute-start | bytes 786440 | tf_op jit(solution)/shard_map/ppermute | solution.py:41
  41.8 14.7 %collective-permute-start.14 = (f32[4,128,128]{2,1,0:T(8,128)S(1)}, f32[4,128,128]{2,1,0:T(8,128)S(1)}, u32[]{:S(2)}, u32[]{:S(2)}) collective-permute-start(f32[4,128,128]{2,1,0:T(8,128)S(1)} %pad_maximum_fusion.1.b_all), channel_id=1, source_target_pairs={{0,96},{96,0},{32,64},{64,32},{1,97},{97,1},{33,65},{65,33},{2,98}... | collective-permute-start | bytes 786440 | tf_op jit(solution)/shard_map/ppermute | solution.py:41
  46.1 12.5 %collective-permute-start.18 = (f32[2,2,128,128]{3,2,1,0:T(8,128)S(1)}, f32[2,2,128,128]{3,2,1,0:T(8,128)S(1)}, u32[]{:S(2)}, u32[]{:S(2)}) collective-permute-start(f32[2,2,128,128]{3,2,1,0:T(8,128)S(1)} %pad_maximum_fusion.2), channel_id=1, source_target_pairs={{0,2},{2,0},{1,3},{3,1},{4,6},{6,4},{5,7},{7,5},{8,10},{10,8},{9,1... | collective-permute-start | bytes 786440 | tf_op jit(solution)/shard_map/ppermute | solution.py:41
  58.5 1.6 %collective-permute-start.15 = (f32[2,2,128,128]{3,2,1,0:T(8,128)S(1)}, f32[2,2,128,128]{3,2,1,0:T(8,128)S(1)}, u32[]{:S(2)}, u32[]{:S(2)}) collective-permute-start(f32[2,2,128,128]{3,2,1,0:T(8,128)S(1)} %get-tuple-element.18), channel_id=1, source_target_pairs={{0,1},{1,0},{2,3},{3,2},{4,5},{5,4},{6,7},{7,6},{8,9},{9,8},{10,11... | collective-permute-start | bytes 786440 | tf_op jit(solution)/shard_map/ppermute | solution.py:41
  61.3 21.2 %all-to-all-start = ((f32[64,16,128]{2,1,0:T(8,128)}), f32[64,16,128]{2,1,0:T(8,128)S(1)}, u32[]{:S(2)}, u32[]{:S(2)}) async-start(f32[64,16,128]{2,1,0:T(8,128)} %bitcast.17), calls=%async_computation | async-start | bytes 1048576 | tf_op jit(solution)/shard_map/all_to_all | solution.py:313
  69.0 8.8 %collective-permute-start.19 = (f32[128,128]{1,0:T(8,128)S(1)}, f32[128,128]{1,0:T(8,128)S(1)}, u32[]{:S(2)}, u32[]{:S(2)}) collective-permute-start(f32[128,128]{1,0:T(8,128)S(1)} %get-tuple-element.28), channel_id=1, source_target_pairs={{0,2},{2,0},{1,3},{3,1},{4,6},{6,4},{5,7},{7,5},{8,10},{10,8},{9,1... | collective-permute-start | bytes 196616 | tf_op jit(solution)/shard_map/ppermute | solution.py:41
  72.1 8.3 %collective-permute-start.20 = (f32[128,128]{1,0:T(8,128)S(1)}, f32[128,128]{1,0:T(8,128)S(1)}, u32[]{:S(2)}, u32[]{:S(2)}) collective-permute-start(f32[128,128]{1,0:T(8,128)S(1)} %get-tuple-element.27), channel_id=1, source_target_pairs={{0,16},{16,0},{1,17},{17,1},{2,18},{18,2},{3,19},{19,3},{4,20},{20... | collective-permute-start | bytes 196616 | tf_op jit(solution)/shard_map/ppermute | solution.py:41
  72.7 8.1 %collective-permute-start.21 = (f32[128,128]{1,0:T(8,128)S(1)}, f32[128,128]{1,0:T(8,128)S(1)}, u32[]{:S(2)}, u32[]{:S(2)}) collective-permute-start(f32[128,128]{1,0:T(8,128)S(1)} %get-tuple-element.26), channel_id=1, source_target_pairs={{0,18},{2,16},{16,2},{18,0},{1,19},{3,17},{17,3},{19,1},{4,22},{6,... | collective-permute-start | bytes 196616 | tf_op jit(solution)/shard_map/ppermute | solution.py:41

commit v2 on v1

--- a/solution.py
+++ b/solution.py
@@ -79,12 +79,20 @@
     counts_hbm,
     ancestors_hbm,
     diag_hbm,
+    mine,
+    g_zl,
+    g_core,
+    band_own,
+    band_other,
     square,
     col_mask,
     row_mask,
     out_mask,
     diag_hi,
     diag_lo,
+    scaled,
+    band_hi,
+    band_lo,
     tile,
     counts,
     ancestors,
@@ -130,63 +138,8 @@
     hi, lo = split(diag[zl])
     diag_hi[...] = hi
     diag_lo[...] = lo
-
-
-def left_factor(diag_hi, diag_lo, row_mask, mine, g_zl, g_core, g_zh, hi_t, lo_t):
-    _, _, _, zh, core = position()
-    pcol = 2 * zh + core
-    quarters = (
-        (mine[...], g_zl[...], pcol),
-        (g_core[0], g_core[1], 2 * zh + 1 - core),
-        (g_zh[0, 0], g_zh[0, 1], 2 - 2 * zh + core),
-        (g_zh[1, 0], g_zh[1, 1], 3 - 2 * zh - core),
-    )
-    scaled = jnp.zeros((2 * Q, W), jnp.float32)
-    for own, partner, quarter in quarters:
-        rows = jnp.concatenate([own, partner], axis=0) * row_mask[...]
-        start = pl.multiple_of(quarter * Q, Q)
-        scaled = scaled + dot3(split(rows), (diag_hi[pl.ds(start, Q), :], diag_lo[pl.ds(start, Q), :]))
-    hi, lo = split(scaled.T)
-    hi_t[...] = hi
-    lo_t[...] = lo
-
-
-def products(
-    band_own,
-    band_other,
-    col_mask,
-    a_all,
-    a_even,
-    a_far,
-    a_odd,
-    b_all,
-    b_even,
-    b_far,
-    b_odd,
-    diag_hi,
-    diag_lo,
-    part_keep,
-    part_send,
-    band_hi,
-    band_lo,
-    panel_hi,
-    panel_lo,
-    turned_hi,
-    turned_lo,
-):
-    x, zl, y, zh, core = position()
-    pieces = {}
-    for outer, refs in enumerate(((a_all, a_even, a_far, a_odd), (b_all, b_even, b_far, b_odd))):
-        for far, ref in enumerate(refs):
-            for near in range(4):
-                xo, q = (near, far) if outer == 0 else (far, near)
-                pieces[outer, xo, q] = ref.at[near]
-    for (stream, xo, q), ref in pieces.items():
-        hi, lo = split(ref[...])
-        rows = slice((2 * xo + stream) * Q, (2 * xo + stream + 1) * Q)
-        cols = slice(q * Q, (q + 1) * Q)
-        panel_hi[rows, cols] = hi
-        panel_lo[rows, cols] = lo
+    quarters = ((mine[...], g_zl[...], pcol), (g_core[0], g_core[1], 2 * zh + 1 - core))
+    scaled[...] = scaled_by(diag_hi, diag_lo, quarters)
     for xo in range(4):
         for stream in range(2):
             side = zl if stream == 0 else 1 - zl
@@ -197,11 +150,60 @@
                 hi, lo = split(ref[:, pl.ds(start, Q)] * mask)
                 band_hi[r * Q : (r + 1) * Q, cols] = hi
                 band_lo[r * Q : (r + 1) * Q, cols] = lo
+
+
+def scaled_by(diag_hi, diag_lo, quarters):
+    total = jnp.zeros((2 * Q, W), jnp.float32)
+    for own, partner, quarter in quarters:
+        rows = jnp.concatenate([own, partner], axis=0)
+        start = pl.multiple_of(quarter * Q, Q)
+        total = total + dot3(split(rows), (diag_hi[pl.ds(start, Q), :], diag_lo[pl.ds(start, Q), :]))
+    return total
+
+
+def left_factor(diag_hi, diag_lo, row_mask, scaled, g_zh, hi_t, lo_t):
+    _, _, _, zh, core = position()
+    quarters = (
+        (g_zh[0, 0], g_zh[0, 1], 2 - 2 * zh + core),
+        (g_zh[1, 0], g_zh[1, 1], 3 - 2 * zh - core),
+    )
+    total = (scaled[...] + scaled_by(diag_hi, diag_lo, quarters)) * row_mask[:, :1]
+    hi, lo = split(total.T)
+    hi_t[...] = hi
+    lo_t[...] = lo
+
+
+def gather_dot(band_hi, band_lo, blocks, xs, stream):
+    slots = [slice((2 * xo + stream) * Q, (2 * xo + stream + 1) * Q) for xo in xs]
+    left = [jnp.concatenate([ref[:, slot] for slot in slots], axis=1) for ref in (band_hi, band_lo)]
+    return dot3(left, split(blocks))
+
+
+def near_products(band_hi, band_lo, a_all, a_even, a_odd, b_all, b_even, b_odd, near):
+    blocks = jnp.concatenate([ref[...].reshape(4 * Q, Q) for ref in (a_all, a_even, a_odd)], axis=1)
+    first = gather_dot(band_hi, band_lo, blocks, range(4), 0)
+    rows = [
+        jnp.concatenate([ref[k] for k in range(4)], axis=1) for ref in (b_all, b_even, b_odd)
+    ]
+    second = gather_dot(band_hi, band_lo, jnp.concatenate(rows, axis=0), (0, 1, 3), 1)
+    near[:, : 2 * Q] = first[:, : 2 * Q] + second[:, : 2 * Q]
+    near[:, 2 * Q : 3 * Q] = second[:, 2 * Q : 3 * Q]
+    near[:, 3 * Q :] = first[:, 2 * Q :] + second[:, 3 * Q :]
+
+
+def products(
+    band_hi, band_lo, near, a_far, b_far, diag_hi, diag_lo, part_keep, part_send, turned_hi, turned_lo, total
+):
+    _, _, y, zh, core = position()
+    row = jnp.concatenate([b_far[k] for k in range(4)], axis=1)
+    total[...] = near[...] + gather_dot(band_hi, band_lo, row, (2,), 1)
+    column = a_far[...].reshape(4 * Q, Q)
+    total[:, 2 * Q : 3 * Q] += gather_dot(band_hi, band_lo, column, range(4), 0)
     for q in range(4):
         start = pl.multiple_of((y ^ q) * Q, Q)
         turned_hi[q * Q : (q + 1) * Q, :] = diag_hi[pl.ds(start, Q), :]
         turned_lo[q * Q : (q + 1) * Q, :] = diag_lo[pl.ds(start, Q), :]
-    product = dot3((band_hi[...], band_lo[...]), (panel_hi[...], panel_lo[...]))
+    product = total[...]
     partial = dot3(split(product), (turned_hi[...], turned_lo[...]))
     for c in range(2):
 
@@ -257,12 +259,24 @@
     b_here = send(other, AXES, route(lambda x, zl, y, c: (x, 1 - zl, c, y)))
     band_other = send(band, "zl", SWAP)
 
-    square, col_mask, row_mask, out_mask, diag_hi, diag_lo = call(
+    a4 = jnp.stack([a_here, send(a_here, "x", EVEN), send(a_here, "x", FAR), send(a_here, "x", ODD)])
+    b4 = jnp.stack([b_here, send(b_here, "y", EVEN), send(b_here, "y", FAR), send(b_here, "y", ODD)])
+    a_even, b_even = send(a4, "y", EVEN), send(b4, "x", EVEN)
+    a_far, b_far = send(a4, "y", FAR), send(b4, "x", FAR)
+    a_odd, b_odd = send(a4, "y", ODD), send(b4, "x", ODD)
+
+    g_zl = send(other, "zl", SWAP)
+    rows = jnp.stack([mine, g_zl])
+    g_core = send(rows, "core", SWAP)
+    g_zh = send(jnp.stack([rows, g_core]), "zh", SWAP)
+    square, _, row_mask, out_mask, diag_hi, diag_lo, scaled, band_hi, band_lo = call(
         early,
-        (f32(2, 16, Q), f32(1, 8 * Q), f32(2 * Q, Q), f32(2, Q, Q), bf16(W, W), bf16(W, W)),
-        [pltpu.with_memory_space_constraint(v, pltpu.HBM) for v in (counts, ancestors, diag_inverse)],
+        (f32(2, 16, Q), f32(1, 8 * Q), f32(2 * Q, Q), f32(2, Q, Q), bf16(W, W), bf16(W, W), f32(2 * Q, W))
+        + (bf16(2 * Q, 8 * Q), bf16(2 * Q, 8 * Q)),
+        [pltpu.with_memory_space_constraint(v, pltpu.HBM) for v in (counts, ancestors, diag_inverse)]
+        + [mine, g_zl, g_core, band, band_other],
         12,
-        in_specs=[pl.BlockSpec(memory_space=pltpu.HBM)] * 3,
+        in_specs=[pl.BlockSpec(memory_space=pltpu.HBM)] * 3 + [ALL_VMEM] * 5,
         scratch=[
             pltpu.VMEM((Q, Q), jnp.float32),
             pltpu.SMEM((2,), jnp.int32),
@@ -271,45 +285,19 @@
             pltpu.SemaphoreType.DMA((3,)),
         ],
     )
-    a4 = jnp.stack(
-        [a_here, send(a_here, "x", EVEN), send(a_here, "x", FAR), send(a_here, "x", ODD)]
-    )
-    b4 = jnp.stack(
-        [b_here, send(b_here, "y", EVEN), send(b_here, "y", FAR), send(b_here, "y", ODD)]
-    )
-    a_even, b_even = send(a4, "y", EVEN), send(b4, "x", EVEN)
-    a_far, b_far = send(a4, "y", FAR), send(b4, "x", FAR)
-    a_odd, b_odd = send(a4, "y", ODD), send(b4, "x", ODD)
-
-    g_zl = send(other, "zl", SWAP)
-    rows = jnp.stack([mine, g_zl])
-    g_core = send(rows, "core", SWAP)
-    g_zh = send(jnp.stack([rows, g_core]), "zh", SWAP)
     left_hi, left_lo = call(
-        left_factor,
-        (bf16(W, 2 * Q), bf16(W, 2 * Q)),
-        (diag_hi, diag_lo, row_mask, mine, g_zl, g_core, g_zh),
-        12,
-    )
+        left_factor, (bf16(W, 2 * Q), bf16(W, 2 * Q)), (diag_hi, diag_lo, row_mask, scaled, g_zh), 12
+    )
+    (near,) = call(near_products, (f32(2 * Q, W),), (band_hi, band_lo, a4, a_even, a_odd, b4, b_even, b_odd), 16)
     part_keep, part_send = call(
         products,
         (f32(2, 2, Q, Q), f32(2, 2, Q, Q)),
-        (
-            (band, band_other, col_mask)
-            + (a4, a_even, a_far, a_odd)
-            + (b4, b_even, b_far, b_odd)
-            + (diag_hi, diag_lo)
-        ),
-        20,
-        scratch=vmem(*[(2 * Q, 8 * Q)] * 2, *[(8 * Q, W)] * 2, *[(W, W)] * 2),
+        (band_hi, band_lo, near, a_far, b_far, diag_hi, diag_lo),
+        16,
+        scratch=vmem(*[(W, W)] * 2) + [pltpu.VMEM((2 * Q, W), jnp.float32)],
     )
     part_got = send(part_send, "core", SWAP)
-    parts, corr = call(
-        correction,
-        (f32(2, 2, Q, Q), f32(32, 2, 16, Q)),
-        (part_keep, part_got, left_hi, left_lo),
-        12,
-    )
+    parts, corr = call(correction, (f32(2, 2, Q, Q), f32(32, 2, 16, Q)), (part_keep, part_got, left_hi, left_lo), 12)
     landed = lax.all_to_all(corr.reshape(64, 16, Q), ("x", "zl", "y", "zh"), 0, 0, tiled=True)
     in_a = send(parts[0, 1], "zh", SWAP)
     in_b = send(parts[1, 0], "zl", SWAP)

time: 83.5 us -> 84.7 us (1.014)
  waiting for transfers between devices: 27.6 us -> 30.1 us
  starting transfers between devices: 46.6 us -> 44.8 us
    ppermute x22, starting transfers between devices: 39 us -> 32.9 us  [send(): return lax.ppermute(x, axes, pairs)]
    all_to_all x1, starting transfers between devices: 7.66 us -> 11.9 us  [step(): lax.all_to_all(corr.reshape(64, 16, Q), ('x', 'zl', 'y', 'zh'), 0, 0, til...]
    ppermute x22, waiting for transfers between devices: 25.8 us -> 29.1 us  [send(): return lax.ppermute(x, axes, pairs)]
    pallas_call x5 -> x6, Pallas kernels: 7.24 us -> 7.78 us  [call(): pl.pallas_call(body, out_shape=out_shape, in_specs=in_specs or [ALL_VMEM]...]
  transfers between devices with their start and end apart: 23 -> 23, of which waited for: 9 -> 11; matrix products, arithmetic and copies ran while one was open for 0% -> 1% of each run, Pallas kernels for 6% -> 7%
where the time goes in v2:
time: 84.7 us; the launch traced here: 84.4 us
  starting transfers between devices  44.8 us (53%)
  waiting for transfers between devices  30.1 us (36%)
  Pallas kernels  7.78 us (9%)
  local copies, waits for them, and re-layouts  0.9 us (1%)
    ppermute x22, starting transfers between devices, send(): return lax.ppermute(x, axes, pairs)  32.9 us
    ppermute x22, waiting for transfers between devices, send(): return lax.ppermute(x, axes, pairs)  29.1 us
    all_to_all x1, starting transfers between devices, step(): lax.all_to_all(corr.reshape(64, 16, Q), ('x', 'zl', 'y', 'zh'), 0, 0, til...  11.9 us
    pallas_call x6, Pallas kernels, call(): pl.pallas_call(body, out_shape=out_shape, in_specs=in_specs or [ALL_VMEM]...  7.78 us
  transfers between devices with their start and end apart: 23, of which 11 were waited for; matrix products, arithmetic and copies ran while one was open for 1% of the time, Pallas kernels for 7%

profile of v2, /device:TPU:0, one launch (start us, length us, event | category | flops | bytes accessed | tf_op | source)
XLA Modules:
  0.0 84.4 jit_solution(360018203856406955)
XLA Ops:
  0.6 2.1 %collective-permute-start.2 = (f32[128,1024]{1,0:T(8,128)}, f32[128,1024]{1,0:T(8,128)S(1)}, u32[]{:S(2)}, u32[]{:S(2)}) collective-permute-start(f32[128,1024]{1,0:T(8,128)} %band_own.1), channel_id=1, source_target_pairs={{0,16},{16,0},{1,17},{17,1},{2,18},{18,2},{3,19},{19,3},{4,20},{20... | collective-permute-start | bytes 1572872 | tf_op jit(solution)/shard_map/ppermute | solution.py:41
  2.7 0.9 %dynamic-slice_bitcast_fusion = (f32[128,128]{1,0:T(8,128)S(1)}, f32[1,128,128]{2,1,0:T(8,128)S(1)}) fusion(f32[2,128,128]{2,1,0:T(8,128)} %param.6, s32[]{:T(128)S(6)} %select_n.8, s32[]{:T(128)S(6)} %select_n.7), kind=kLoop, calls=%fused_computation.8 | loop fusion | bytes 262152 | tf_op jit(solution)/shard_map/jit(dynamic_index_in_dim)/squeeze | solution.py:45
  3.8 12.5 %collective-permute-done.9 = f32[128,128]{1,0:T(8,128)S(1)} collective-permute-done((f32[128,128]{1,0:T(8,128)S(1)}, f32[128,128]{1,0:T(8,128)S(1)}, u32[]{:S(2)}, u32[]{:S(2)}) %collective-permute-start.9) | collective-permute-done | bytes 65568 | tf_op jit(solution)/shard_map/ppermute | solution.py:41
  16.3 4.7 %collective-permute-start.11 = (f32[128,128]{1,0:T(8,128)S(1)}, f32[128,128]{1,0:T(8,128)S(1)}, u32[]{:S(2)}, u32[]{:S(2)}) collective-permute-start(f32[128,128]{1,0:T(8,128)S(1)} %collective-permute-done.9), channel_id=1, source_target_pairs={{0,8},{8,0},{4,12},{12,4},{1,9},{9,1},{5,13},{13,5},{2,10},{10,2},... | collective-permute-start | bytes 196616 | tf_op jit(solution)/shard_map/ppermute | solution.py:41
  21.0 1.7 %collective-permute-start = (f32[128,128]{1,0:T(8,128)S(1)}, f32[128,128]{1,0:T(8,128)S(1)}, u32[]{:S(2)}, u32[]{:S(2)}) collective-permute-start(f32[128,128]{1,0:T(8,128)S(1)} %get-tuple-element.36), channel_id=1, source_target_pairs={{0,16},{16,0},{1,17},{17,1},{2,18},{18,2},{3,19},{19,3},{4,20},{20... | collective-permute-start | bytes 196616 | tf_op jit(solution)/shard_map/ppermute | solution.py:41
  23.9 1.6 %collective-permute-start.13 = (f32[4,128,128]{2,1,0:T(8,128)S(1)}, f32[4,128,128]{2,1,0:T(8,128)S(1)}, u32[]{:S(2)}, u32[]{:S(2)}) collective-permute-start(f32[4,128,128]{2,1,0:T(8,128)S(1)} %pad_maximum_fusion.1.b_all), channel_id=1, source_target_pairs={{0,32},{32,0},{64,96},{96,64},{1,33},{33,1},{65,97},{97,65},{2,34}... | collective-permute-start | bytes 786440 | tf_op jit(solution)/shard_map/ppermute | solution.py:41
  26.1 3.0 %collective-permute-start.5 = (f32[128,128]{1,0:T(8,128)S(1)}, f32[128,128]{1,0:T(8,128)S(1)}, u32[]{:S(2)}, u32[]{:S(2)}) collective-permute-start(f32[128,128]{1,0:T(8,128)S(1)} %collective-permute-done.3), channel_id=1, source_target_pairs={{0,64},{64,0},{32,96},{96,32},{1,65},{65,1},{33,97},{97,33},{2,66}... | collective-permute-start | bytes 196616 | tf_op jit(solution)/shard_map/ppermute | solution.py:41
  29.1 1.1 %collective-permute-start.6 = (f32[128,128]{1,0:T(8,128)S(1)}, f32[128,128]{1,0:T(8,128)S(1)}, u32[]{:S(2)}, u32[]{:S(2)}) collective-permute-start(f32[128,128]{1,0:T(8,128)S(1)} %collective-permute-done.3), channel_id=1, source_target_pairs={{0,96},{96,0},{32,64},{64,32},{1,97},{97,1},{33,65},{65,33},{2,98}... | collective-permute-start | bytes 196616 | tf_op jit(solution)/shard_map/ppermute | solution.py:41
  30.2 4.3 %collective-permute-done.4 = f32[128,128]{1,0:T(8,128)S(1)} collective-permute-done((f32[128,128]{1,0:T(8,128)S(1)}, f32[128,128]{1,0:T(8,128)S(1)}, u32[]{:S(2)}, u32[]{:S(2)}) %collective-permute-start.4) | collective-permute-done | bytes 65568 | tf_op jit(solution)/shard_map/ppermute | solution.py:41
  34.6 2.9 %collective-permute-done.5 = f32[128,128]{1,0:T(8,128)S(1)} collective-permute-done((f32[128,128]{1,0:T(8,128)S(1)}, f32[128,128]{1,0:T(8,128)S(1)}, u32[]{:S(2)}, u32[]{:S(2)}) %collective-permute-start.5) | collective-permute-done | bytes 65568 | tf_op jit(solution)/shard_map/ppermute | solution.py:41
  38.1 6.3 %collective-permute-start.8 = (f32[4,128,128]{2,1,0:T(8,128)S(1)}, f32[4,128,128]{2,1,0:T(8,128)S(1)}, u32[]{:S(2)}, u32[]{:S(2)}) collective-permute-start(f32[4,128,128]{2,1,0:T(8,128)S(1)} %pad_maximum_fusion.a_all), channel_id=1, source_target_pairs={{0,12},{12,0},{4,8},{8,4},{1,13},{13,1},{5,9},{9,5},{2,14},{14,2},... | collective-permute-start | bytes 786440 | tf_op jit(solution)/shard_map/ppermute | solution.py:41
  44.8 1.7 %collective-permute-start.16 = (f32[4,128,128]{2,1,0:T(8,128)S(1)}, f32[4,128,128]{2,1,0:T(8,128)S(1)}, u32[]{:S(2)}, u32[]{:S(2)}) collective-permute-start(f32[4,128,128]{2,1,0:T(8,128)S(1)} %pad_maximum_fusion.1.b_all), channel_id=1, source_target_pairs={{0,64},{64,0},{32,96},{96,32},{1,65},{65,1},{33,97},{97,33},{2,66}... | collective-permute-start | bytes 786440 | tf_op jit(solution)/shard_map/ppermute | solution.py:41
  46.6 3.2 %shard_map.68 = (f32[2,16,128]{2,1,0:T(8,128)S(1)}, f32[1,1024]{1,0:T(1,128)}, f32[256,128]{1,0:T(8,128)S(1)}, f32[2,128,128]{2,1,0:T(8,128)S(1)}, bf16[512,512]...) custom-call(s32[2]{0:T(128)} %counts_hbm.1, ...), custom_call_target="tpu_custom_call" | custom-call | tf_op jit(solution)/shard_map/pallas_call | solution.py:68
  49.8 3.9 %collective-permute-start.18 = (f32[2,2,128,128]{3,2,1,0:T(8,128)S(1)}, f32[2,2,128,128]{3,2,1,0:T(8,128)S(1)}, u32[]{:S(2)}, u32[]{:S(2)}) collective-permute-start(f32[2,2,128,128]{3,2,1,0:T(8,128)S(1)} %pad_maximum_fusion.2), channel_id=1, source_target_pairs={{0,2},{2,0},{1,3},{3,1},{4,6},{6,4},{5,7},{7,5},{8,10},{10,8},{9,1... | collective-permute-start | bytes 786440 | tf_op jit(solution)/shard_map/ppermute | solution.py:41
  53.7 1.3 %collective-permute-done.8.a_odd = f32[4,128,128]{2,1,0:T(8,128)S(1)} collective-permute-done((f32[4,128,128]{2,1,0:T(8,128)S(1)}, f32[4,128,128]{2,1,0:T(8,128)S(1)}, u32[]{:S(2)}, u32[]{:S(2)}) %collective-permute-start.8) | collective-permute-done | bytes 262176 | tf_op jit(solution)/shard_map/ppermute | solution.py:41
  54.9 1.0 %shard_map.69.near = f32[256,512]{1,0:T(8,128)S(1)} custom-call(bf16[256,1024]{1,0:T(8,128)(2,1)S(1)} %get-tuple-element.16.band_hi, bf16[256,1024]{1,0:T(8,128)(2,1)S(1)} %get-tuple-element.17.band_lo, f32[4,128,128]{2,1,0:T(8,128)S(1)} %pad_maximum_fusion.a_all, f32[4,128,128]{2,1,0:T(8,128)S(1)} %collective-permute-done.7.a_even, ...), custom_call_target="tpu_custom_call" | custom-call | tf_op jit(solution)/shard_map/pallas_call | solution.py:68
  56.0 1.0 %shard_map.70 = (f32[2,2,128,128]{3,2,1,0:T(8,128)S(1)}, f32[2,2,128,128]{3,2,1,0:T(8,128)S(1)}) custom-call(bf16[256,1024]{1,0:T(8,128)(2,1)S(1)} %get-tuple-element.16.band_hi, bf16[256,1024]{1,0:T(8,128)(2,1)S(1)} %get-tuple-element.17.band_lo, f32[256,512]{1,0:T(8,128)S(1)} %shard_map.69.near, f32[4,128,128]{2,1,0:T(8,128)S(1)} %collective-permute-done.15.a_far, ...), custom_call_target="tpu_custom_call" | custom-call | tf_op jit(solution)/shard_map/pallas_call | solution.py:68
  57.1 0.9 %collective-permute-done.18.g_zh = f32[2,2,128,128]{3,2,1,0:T(8,128)S(1)} collective-permute-done((f32[2,2,128,128]{3,2,1,0:T(8,128)S(1)}, f32[2,2,128,128]{3,2,1,0:T(8,128)S(1)}, u32[]{:S(2)}, u32[]{:S(2)}) %collective-permute-start.18) | collective-permute-done | bytes 262176 | tf_op jit(solution)/shard_map/ppermute | solution.py:41
  58.7 1.2 %shard_map.72 = (f32[2,2,128,128]{3,2,1,0:T(8,128)S(1)}, f32[32,2,16,128]{3,2,1,0:T(8,128)}) custom-call(f32[2,2,128,128]{3,2,1,0:T(8,128)S(1)} %get-tuple-element.20.part_keep, f32[2,2,128,128]{3,2,1,0:T(8,128)S(1)} %collective-permute-done.17.part_got, bf16[512,256]{1,0:T(8,128)(2,1)S(1)} %get-tuple-element.24.left_hi, ...), custom_call_target="tpu_custom_call" | custom-call | tf_op jit(solution)/shard_map/pallas_call | solution.py:68
  59.9 11.9 %all-to-all-start = ((f32[64,16,128]{2,1,0:T(8,128)}), f32[64,16,128]{2,1,0:T(8,128)S(1)}, u32[]{:S(2)}, u32[]{:S(2)}) async-start(f32[64,16,128]{2,1,0:T(8,128)} %bitcast.17), calls=%async_computation | async-start | bytes 1048576 | tf_op jit(solution)/shard_map/all_to_all | solution.py:301
  71.9 3.2 %collective-permute-start.19 = (f32[128,128]{1,0:T(8,128)S(1)}, f32[128,128]{1,0:T(8,128)S(1)}, u32[]{:S(2)}, u32[]{:S(2)}) collective-permute-start(f32[128,128]{1,0:T(8,128)S(1)} %get-tuple-element.32), channel_id=1, source_target_pairs={{0,2},{2,0},{1,3},{3,1},{4,6},{6,4},{5,7},{7,5},{8,10},{10,8},{9,1... | collective-permute-start | bytes 196616 | tf_op jit(solution)/shard_map/ppermute | solution.py:41
  76.2 5.0 %collective-permute-done.19.in_a = f32[128,128]{1,0:T(8,128)S(1)} collective-permute-done((f32[128,128]{1,0:T(8,128)S(1)}, f32[128,128]{1,0:T(8,128)S(1)}, u32[]{:S(2)}, u32[]{:S(2)}) %collective-permute-start.19) | collective-permute-done | bytes 65568 | tf_op jit(solution)/shard_map/ppermute | solution.py:41
  81.8 1.0 %collective-permute-done.21.in_c = f32[128,128]{1,0:T(8,128)S(1)} collective-permute-done((f32[128,128]{1,0:T(8,128)S(1)}, f32[128,128]{1,0:T(8,128)S(1)}, u32[]{:S(2)}, u32[]{:S(2)}) %collective-permute-start.21) | collective-permute-done | bytes 65568 | tf_op jit(solution)/shard_map/ppermute | solution.py:41
  82.8 0.9 %all-to-all-done = f32[64,16,128]{2,1,0:T(8,128)S(1)} async-done(((f32[64,16,128]{2,1,0:T(8,128)}), f32[64,16,128]{2,1,0:T(8,128)S(1)}, u32[]{:S(2)}, u32[]{:S(2)}) %all-to-all-start) | async-done | bytes 524320 | tf_op jit(solution)/shard_map/all_to_all | solution.py:301
  (36 shorter events, 6.4 us)
Async XLA Ops:
  0.6 45.9 %copy-start = (f32[128,1024]{1,0:T(8,128)S(1)}, f32[128,1024]{1,0:T(8,128)}, u32[]{:S(2)}) copy-start(f32[128,1024]{1,0:T(8,128)} %band_own.1) | copy-start | bytes 1572868
  0.6 44.2 %collective-permute-start.2 = (f32[128,1024]{1,0:T(8,128)}, f32[128,1024]{1,0:T(8,128)S(1)}, u32[]{:S(2)}, u32[]{:S(2)}) collective-permute-start(f32[128,1024]{1,0:T(8,128)} %band_own.1), channel_id=1, source_target_pairs={{0,16},{16,0},{1,17},{17,1},{2,18},{18,2},{3,19},{19,3},{4,20},{20... | collective-permute-start | bytes 1572872 | tf_op jit(solution)/shard_map/ppermute | solution.py:41
  3.6 12.7 %collective-permute-start.9 = (f32[128,128]{1,0:T(8,128)S(1)}, f32[128,128]{1,0:T(8,128)S(1)}, u32[]{:S(2)}, u32[]{:S(2)}) collective-permute-start(f32[128,128]{1,0:T(8,128)S(1)} %get-tuple-element.36), channel_id=1, source_target_pairs={{0,16},{1,20},{2,24},{3,28},{4,17},{5,21},{6,25},{7,29},{8,18},{9,... | collective-permute-start | bytes 196616 | tf_op jit(solution)/shard_map/ppermute | solution.py:41
  16.3 6.4 %collective-permute-start.12 = (f32[128,128]{1,0:T(8,128)S(1)}, f32[128,128]{1,0:T(8,128)S(1)}, u32[]{:S(2)}, u32[]{:S(2)}) collective-permute-start(f32[128,128]{1,0:T(8,128)S(1)} %collective-permute-done.9), channel_id=1, source_target_pairs={{0,12},{12,0},{4,8},{8,4},{1,13},{13,1},{5,9},{9,5},{2,14},{14,2},... | collective-permute-start | bytes 196616 | tf_op jit(solution)/shard_map/ppermute | solution.py:41
  16.3 7.1 %collective-permute-start.10 = (f32[128,128]{1,0:T(8,128)S(1)}, f32[128,128]{1,0:T(8,128)S(1)}, u32[]{:S(2)}, u32[]{:S(2)}) collective-permute-start(f32[128,128]{1,0:T(8,128)S(1)} %collective-permute-done.9), channel_id=1, source_target_pairs={{0,4},{4,0},{8,12},{12,8},{1,5},{5,1},{9,13},{13,9},{2,6},{6,2},{1... | collective-permute-start | bytes 196616 | tf_op jit(solution)/shard_map/ppermute | solution.py:41
  16.3 7.6 %collective-permute-start.11 = (f32[128,128]{1,0:T(8,128)S(1)}, f32[128,128]{1,0:T(8,128)S(1)}, u32[]{:S(2)}, u32[]{:S(2)}) collective-permute-start(f32[128,128]{1,0:T(8,128)S(1)} %collective-permute-done.9), channel_id=1, source_target_pairs={{0,8},{8,0},{4,12},{12,4},{1,9},{9,1},{5,13},{13,5},{2,10},{10,2},... | collective-permute-start | bytes 196616 | tf_op jit(solution)/shard_map/ppermute | solution.py:41
  21.0 8.1 %collective-permute-start = (f32[128,128]{1,0:T(8,128)S(1)}, f32[128,128]{1,0:T(8,128)S(1)}, u32[]{:S(2)}, u32[]{:S(2)}) collective-permute-start(f32[128,128]{1,0:T(8,128)S(1)} %get-tuple-element.36), channel_id=1, source_target_pairs={{0,16},{16,0},{1,17},{17,1},{2,18},{18,2},{3,19},{19,3},{4,20},{20... | collective-permute-start | bytes 196616 | tf_op jit(solution)/shard_map/ppermute | solution.py:41
  22.7 2.8 %collective-permute-start.3 = (f32[128,128]{1,0:T(8,128)S(1)}, f32[128,128]{1,0:T(8,128)S(1)}, u32[]{:S(2)}, u32[]{:S(2)}) collective-permute-start(f32[128,128]{1,0:T(8,128)S(1)} %bitcast.26), channel_id=1, source_target_pairs={{0,0},{1,4},{2,8},{3,12},{4,1},{5,5},{6,9},{7,13},{8,2},{9,6},{10,... | collective-permute-start | bytes 196616 | tf_op jit(solution)/shard_map/ppermute | solution.py:41
  23.9 20.4 %collective-permute-start.13 = (f32[4,128,128]{2,1,0:T(8,128)S(1)}, f32[4,128,128]{2,1,0:T(8,128)S(1)}, u32[]{:S(2)}, u32[]{:S(2)}) collective-permute-start(f32[4,128,128]{2,1,0:T(8,128)S(1)} %pad_maximum_fusion.1.b_all), channel_id=1, source_target_pairs={{0,32},{32,0},{64,96},{96,64},{1,33},{33,1},{65,97},{97,65},{2,34}... | collective-permute-start | bytes 786440 | tf_op jit(solution)/shard_map/ppermute | solution.py:41
  25.5 9.1 %collective-permute-start.4 = (f32[128,128]{1,0:T(8,128)S(1)}, f32[128,128]{1,0:T(8,128)S(1)}, u32[]{:S(2)}, u32[]{:S(2)}) collective-permute-start(f32[128,128]{1,0:T(8,128)S(1)} %collective-permute-done.3), channel_id=1, source_target_pairs={{0,32},{32,0},{64,96},{96,64},{1,33},{33,1},{65,97},{97,65},{2,34}... | collective-permute-start | bytes 196616 | tf_op jit(solution)/shard_map/ppermute | solution.py:41
  26.1 11.4 %collective-permute-start.5 = (f32[128,128]{1,0:T(8,128)S(1)}, f32[128,128]{1,0:T(8,128)S(1)}, u32[]{:S(2)}, u32[]{:S(2)}) collective-permute-start(f32[128,128]{1,0:T(8,128)S(1)} %collective-permute-done.3), channel_id=1, source_target_pairs={{0,64},{64,0},{32,96},{96,32},{1,65},{65,1},{33,97},{97,33},{2,66}... | collective-permute-start | bytes 196616 | tf_op jit(solution)/shard_map/ppermute | solution.py:41
  29.1 8.9 %collective-permute-start.6 = (f32[128,128]{1,0:T(8,128)S(1)}, f32[128,128]{1,0:T(8,128)S(1)}, u32[]{:S(2)}, u32[]{:S(2)}) collective-permute-start(f32[128,128]{1,0:T(8,128)S(1)} %collective-permute-done.3), channel_id=1, source_target_pairs={{0,96},{96,0},{32,64},{64,32},{1,97},{97,1},{33,65},{65,33},{2,98}... | collective-permute-start | bytes 196616 | tf_op jit(solution)/shard_map/ppermute | solution.py:41
  34.6 3.5 %collective-permute-start.1 = (f32[2,128,128]{2,1,0:T(8,128)S(1)}, f32[2,128,128]{2,1,0:T(8,128)S(1)}, u32[]{:S(2)}, u32[]{:S(2)}) collective-permute-start(f32[2,128,128]{2,1,0:T(8,128)S(1)} %get-tuple-element.35), channel_id=1, source_target_pairs={{0,1},{1,0},{2,3},{3,2},{4,5},{5,4},{6,7},{7,6},{8,9},{9,8},{10,11... | collective-permute-start | bytes 393224 | tf_op jit(solution)/shard_map/ppermute | solution.py:41
  37.5 12.3 %collective-permute-start.14 = (f32[4,128,128]{2,1,0:T(8,128)S(1)}, f32[4,128,128]{2,1,0:T(8,128)S(1)}, u32[]{:S(2)}, u32[]{:S(2)}) collective-permute-start(f32[4,128,128]{2,1,0:T(8,128)S(1)} %pad_maximum_fusion.1.b_all), channel_id=1, source_target_pairs={{0,96},{96,0},{32,64},{64,32},{1,97},{97,1},{33,65},{65,33},{2,98}... | collective-permute-start | bytes 786440 | tf_op jit(solution)/shard_map/ppermute | solution.py:41
  38.0 15.7 %collective-permute-start.7 = (f32[4,128,128]{2,1,0:T(8,128)S(1)}, f32[4,128,128]{2,1,0:T(8,128)S(1)}, u32[]{:S(2)}, u32[]{:S(2)}) collective-permute-start(f32[4,128,128]{2,1,0:T(8,128)S(1)} %pad_maximum_fusion.a_all), channel_id=1, source_target_pairs={{0,4},{4,0},{8,12},{12,8},{1,5},{5,1},{9,13},{13,9},{2,6},{6,2},{1... | collective-permute-start | bytes 786440 | tf_op jit(solution)/shard_map/ppermute | solution.py:41
  38.1 16.8 %collective-permute-start.8 = (f32[4,128,128]{2,1,0:T(8,128)S(1)}, f32[4,128,128]{2,1,0:T(8,128)S(1)}, u32[]{:S(2)}, u32[]{:S(2)}) collective-permute-start(f32[4,128,128]{2,1,0:T(8,128)S(1)} %pad_maximum_fusion.a_all), channel_id=1, source_target_pairs={{0,12},{12,0},{4,8},{8,4},{1,13},{13,1},{5,9},{9,5},{2,14},{14,2},... | collective-permute-start | bytes 786440 | tf_op jit(solution)/shard_map/ppermute | solution.py:41
  44.4 11.7 %collective-permute-start.15 = (f32[4,128,128]{2,1,0:T(8,128)S(1)}, f32[4,128,128]{2,1,0:T(8,128)S(1)}, u32[]{:S(2)}, u32[]{:S(2)}) collective-permute-start(f32[4,128,128]{2,1,0:T(8,128)S(1)} %pad_maximum_fusion.a_all), channel_id=1, source_target_pairs={{0,8},{8,0},{4,12},{12,4},{1,9},{9,1},{5,13},{13,5},{2,10},{10,2},... | collective-permute-start | bytes 786440 | tf_op jit(solution)/shard_map/ppermute | solution.py:41
  44.8 11.2 %collective-permute-start.16 = (f32[4,128,128]{2,1,0:T(8,128)S(1)}, f32[4,128,128]{2,1,0:T(8,128)S(1)}, u32[]{:S(2)}, u32[]{:S(2)}) collective-permute-start(f32[4,128,128]{2,1,0:T(8,128)S(1)} %pad_maximum_fusion.1.b_all), channel_id=1, source_target_pairs={{0,64},{64,0},{32,96},{96,32},{1,65},{65,1},{33,97},{97,33},{2,66}... | collective-permute-start | bytes 786440 | tf_op jit(solution)/shard_map/ppermute | solution.py:41
  49.8 8.2 %collective-permute-start.18 = (f32[2,2,128,128]{3,2,1,0:T(8,128)S(1)}, f32[2,2,128,128]{3,2,1,0:T(8,128)S(1)}, u32[]{:S(2)}, u32[]{:S(2)}) collective-permute-start(f32[2,2,128,128]{3,2,1,0:T(8,128)S(1)} %pad_maximum_fusion.2), channel_id=1, source_target_pairs={{0,2},{2,0},{1,3},{3,1},{4,6},{6,4},{5,7},{7,5},{8,10},{10,8},{9,1... | collective-permute-start | bytes 786440 | tf_op jit(solution)/shard_map/ppermute | solution.py:41
  57.1 1.7 %collective-permute-start.17 = (f32[2,2,128,128]{3,2,1,0:T(8,128)S(1)}, f32[2,2,128,128]{3,2,1,0:T(8,128)S(1)}, u32[]{:S(2)}, u32[]{:S(2)}) collective-permute-start(f32[2,2,128,128]{3,2,1,0:T(8,128)S(1)} %get-tuple-element.21), channel_id=1, source_target_pairs={{0,1},{1,0},{2,3},{3,2},{4,5},{5,4},{6,7},{7,6},{8,9},{9,8},{10,11... | collective-permute-start | bytes 786440 | tf_op jit(solution)/shard_map/ppermute | solution.py:41
  59.9 23.8 %all-to-all-start = ((f32[64,16,128]{2,1,0:T(8,128)}), f32[64,16,128]{2,1,0:T(8,128)S(1)}, u32[]{:S(2)}, u32[]{:S(2)}) async-start(f32[64,16,128]{2,1,0:T(8,128)} %bitcast.17), calls=%async_computation | async-start | bytes 1048576 | tf_op jit(solution)/shard_map/all_to_all | solution.py:301
  71.9 9.4 %collective-permute-start.19 = (f32[128,128]{1,0:T(8,128)S(1)}, f32[128,128]{1,0:T(8,128)S(1)}, u32[]{:S(2)}, u32[]{:S(2)}) collective-permute-start(f32[128,128]{1,0:T(8,128)S(1)} %get-tuple-element.32), channel_id=1, source_target_pairs={{0,2},{2,0},{1,3},{3,1},{4,6},{6,4},{5,7},{7,5},{8,10},{10,8},{9,1... | collective-permute-start | bytes 196616 | tf_op jit(solution)/shard_map/ppermute | solution.py:41
  75.0 6.8 %collective-permute-start.20 = (f32[128,128]{1,0:T(8,128)S(1)}, f32[128,128]{1,0:T(8,128)S(1)}, u32[]{:S(2)}, u32[]{:S(2)}) collective-permute-start(f32[128,128]{1,0:T(8,128)S(1)} %get-tuple-element.31), channel_id=1, source_target_pairs={{0,16},{16,0},{1,17},{17,1},{2,18},{18,2},{3,19},{19,3},{4,20},{20... | collective-permute-start | bytes 196616 | tf_op jit(solution)/shard_map/ppermute | solution.py:41
  75.6 7.2 %collective-permute-start.21 = (f32[128,128]{1,0:T(8,128)S(1)}, f32[128,128]{1,0:T(8,128)S(1)}, u32[]{:S(2)}, u32[]{:S(2)}) collective-permute-start(f32[128,128]{1,0:T(8,128)S(1)} %get-tuple-element.30), channel_id=1, source_target_pairs={{0,18},{2,16},{16,2},{18,0},{1,19},{3,17},{17,3},{19,1},{4,22},{6,... | collective-permute-start | bytes 196616 | tf_op jit(solution)/shard_map/ppermute | solution.py:41

commit v3 on v2

--- a/solution.py
+++ b/solution.py
@@ -173,37 +173,44 @@
     lo_t[...] = lo
 
 
-def gather_dot(band_hi, band_lo, blocks, xs, stream):
-    slots = [slice((2 * xo + stream) * Q, (2 * xo + stream + 1) * Q) for xo in xs]
-    left = [jnp.concatenate([ref[:, slot] for slot in slots], axis=1) for ref in (band_hi, band_lo)]
-    return dot3(left, split(blocks))
-
-
-def near_products(band_hi, band_lo, a_all, a_even, a_odd, b_all, b_even, b_odd, near):
-    blocks = jnp.concatenate([ref[...].reshape(4 * Q, Q) for ref in (a_all, a_even, a_odd)], axis=1)
-    first = gather_dot(band_hi, band_lo, blocks, range(4), 0)
-    rows = [
-        jnp.concatenate([ref[k] for k in range(4)], axis=1) for ref in (b_all, b_even, b_odd)
-    ]
-    second = gather_dot(band_hi, band_lo, jnp.concatenate(rows, axis=0), (0, 1, 3), 1)
-    near[:, : 2 * Q] = first[:, : 2 * Q] + second[:, : 2 * Q]
-    near[:, 2 * Q : 3 * Q] = second[:, 2 * Q : 3 * Q]
-    near[:, 3 * Q :] = first[:, 2 * Q :] + second[:, 3 * Q :]
-
-
 def products(
-    band_hi, band_lo, near, a_far, b_far, diag_hi, diag_lo, part_keep, part_send, turned_hi, turned_lo, total
+    band_hi,
+    band_lo,
+    a_all,
+    a_even,
+    a_far,
+    a_odd,
+    b_all,
+    b_even,
+    b_far,
+    b_odd,
+    diag_hi,
+    diag_lo,
+    part_keep,
+    part_send,
+    panel_hi,
+    panel_lo,
+    turned_hi,
+    turned_lo,
 ):
     _, _, y, zh, core = position()
-    row = jnp.concatenate([b_far[k] for k in range(4)], axis=1)
-    total[...] = near[...] + gather_dot(band_hi, band_lo, row, (2,), 1)
-    column = a_far[...].reshape(4 * Q, Q)
-    total[:, 2 * Q : 3 * Q] += gather_dot(band_hi, band_lo, column, range(4), 0)
+    pieces = {}
+    for outer, refs in enumerate(((a_all, a_even, a_far, a_odd), (b_all, b_even, b_far, b_odd))):
+        for far, ref in enumerate(refs):
+            for near in range(4):
+                xo, q = (near, far) if outer == 0 else (far, near)
+                pieces[outer, xo, q] = ref.at[near]
+    for (stream, xo, q), ref in pieces.items():
+        hi, lo = split(ref[...])
+        rows = slice((2 * xo + stream) * Q, (2 * xo + stream + 1) * Q)
+        cols = slice(q * Q, (q + 1) * Q)
+        panel_hi[rows, cols] = hi
+        panel_lo[rows, cols] = lo
     for q in range(4):
         start = pl.multiple_of((y ^ q) * Q, Q)
         turned_hi[q * Q : (q + 1) * Q, :] = diag_hi[pl.ds(start, Q), :]
         turned_lo[q * Q : (q + 1) * Q, :] = diag_lo[pl.ds(start, Q), :]
-    product = total[...]
+    product = dot3((band_hi[...], band_lo[...]), (panel_hi[...], panel_lo[...]))
     partial = dot3(split(product), (turned_hi[...], turned_lo[...]))
     for c in range(2):
 
@@ -259,8 +266,12 @@
     b_here = send(other, AXES, route(lambda x, zl, y, c: (x, 1 - zl, c, y)))
     band_other = send(band, "zl", SWAP)
 
-    a4 = jnp.stack([a_here, send(a_here, "x", EVEN), send(a_here, "x", FAR), send(a_here, "x", ODD)])
-    b4 = jnp.stack([b_here, send(b_here, "y", EVEN), send(b_here, "y", FAR), send(b_here, "y", ODD)])
+    a4 = jnp.stack(
+        [a_here, send(a_here, "x", EVEN), send(a_here, "x", FAR), send(a_here, "x", ODD)]
+    )
+    b4 = jnp.stack(
+        [b_here, send(b_here, "y", EVEN), send(b_here, "y", FAR), send(b_here, "y", ODD)]
+    )
     a_even, b_even = send(a4, "y", EVEN), send(b4, "x", EVEN)
     a_far, b_far = send(a4, "y", FAR), send(b4, "x", FAR)
     a_odd, b_odd = send(a4, "y", ODD), send(b4, "x", ODD)
@@ -286,18 +297,30 @@
         ],
     )
     left_hi, left_lo = call(
-        left_factor, (bf16(W, 2 * Q), bf16(W, 2 * Q)), (diag_hi, diag_lo, row_mask, scaled, g_zh), 12
-    )
-    (near,) = call(near_products, (f32(2 * Q, W),), (band_hi, band_lo, a4, a_even, a_odd, b4, b_even, b_odd), 16)
+        left_factor,
+        (bf16(W, 2 * Q), bf16(W, 2 * Q)),
+        (diag_hi, diag_lo, row_mask, scaled, g_zh),
+        12,
+    )
     part_keep, part_send = call(
         products,
         (f32(2, 2, Q, Q), f32(2, 2, Q, Q)),
-        (band_hi, band_lo, near, a_far, b_far, diag_hi, diag_lo),
-        16,
-        scratch=vmem(*[(W, W)] * 2) + [pltpu.VMEM((2 * Q, W), jnp.float32)],
+        (
+            (band_hi, band_lo)
+            + (a4, a_even, a_far, a_odd)
+            + (b4, b_even, b_far, b_odd)
+            + (diag_hi, diag_lo)
+        ),
+        20,
+        scratch=vmem(*[(8 * Q, W)] * 2, *[(W, W)] * 2),
     )
     part_got = send(part_send, "core", SWAP)
-    parts, corr = call(correction, (f32(2, 2, Q, Q), f32(32, 2, 16, Q)), (part_keep, part_got, left_hi, left_lo), 12)
+    parts, corr = call(
+        correction,
+        (f32(2, 2, Q, Q), f32(32, 2, 16, Q)),
+        (part_keep, part_got, left_hi, left_lo),
+        12,
+    )
     landed = lax.all_to_all(corr.reshape(64, 16, Q), ("x", "zl", "y", "zh"), 0, 0, tiled=True)
     in_a = send(parts[0, 1], "zh", SWAP)
     in_b = send(parts[1, 0], "zl", SWAP)

time: 84.7 us -> 85.6 us (1.011)
  waiting for transfers between devices: 30.1 us -> 36.3 us
  starting transfers between devices: 44.8 us -> 39.9 us
    ppermute x22, waiting for transfers between devices: 29.1 us -> 34.6 us  [send(): return lax.ppermute(x, axes, pairs)]
    all_to_all x1, starting transfers between devices: 11.9 us -> 6.75 us  [step(): lax.all_to_all(corr.reshape(64, 16, Q), ('x', 'zl', 'y', 'zh'), 0, 0, til...]
    pallas_call x6 -> x5, Pallas kernels: 7.78 us -> 7.38 us  [call(): pl.pallas_call(body, out_shape=out_shape, in_specs=in_specs or [ALL_VMEM]...]
  transfers between devices with their start and end apart: 23 -> 23, of which waited for: 11 -> 11; matrix products, arithmetic and copies ran while one was open for 1% -> 1% of each run, Pallas kernels for 7% -> 6%
where the time goes in v3:
time: 85.6 us; the launch traced here: 85.4 us
  starting transfers between devices  39.9 us (47%)
  waiting for transfers between devices  36.3 us (42%)
  Pallas kernels  7.38 us (9%)
  local copies, waits for them, and re-layouts  0.9 us (1%)
    ppermute x22, waiting for transfers between devices, send(): return lax.ppermute(x, axes, pairs)  34.6 us
    ppermute x22, starting transfers between devices, send(): return lax.ppermute(x, axes, pairs)  33.1 us
    pallas_call x5, Pallas kernels, call(): pl.pallas_call(body, out_shape=out_shape, in_specs=in_specs or [ALL_VMEM]...  7.38 us
    all_to_all x1, starting transfers between devices, step(): lax.all_to_all(corr.reshape(64, 16, Q), ('x', 'zl', 'y', 'zh'), 0, 0, til...  6.75 us
    all_to_all x1, waiting for transfers between devices, step(): lax.all_to_all(corr.reshape(64, 16, Q), ('x', 'zl', 'y', 'zh'), 0, 0, til...  1.75 us
  transfers between devices with their start and end apart: 23, of which 11 were waited for; matrix products, arithmetic and copies ran while one was open for 1% of the time, Pallas kernels for 6%

profile of v3, /device:TPU:0, one launch (start us, length us, event | category | flops | bytes accessed | tf_op | source)
XLA Modules:
  0.0 85.4 jit_solution(13989395947529916172)
XLA Ops:
  0.6 2.1 %collective-permute-start.2 = (f32[128,1024]{1,0:T(8,128)}, f32[128,1024]{1,0:T(8,128)S(1)}, u32[]{:S(2)}, u32[]{:S(2)}) collective-permute-start(f32[128,1024]{1,0:T(8,128)} %band_own.1), channel_id=1, source_target_pairs={{0,16},{16,0},{1,17},{17,1},{2,18},{18,2},{3,19},{19,3},{4,20},{20... | collective-permute-start | bytes 1572872 | tf_op jit(solution)/shard_map/ppermute | solution.py:41
  2.7 0.9 %dynamic-slice_bitcast_fusion = (f32[128,128]{1,0:T(8,128)S(1)}, f32[1,128,128]{2,1,0:T(8,128)S(1)}) fusion(f32[2,128,128]{2,1,0:T(8,128)} %param.6, s32[]{:T(128)S(6)} %select_n.8, s32[]{:T(128)S(6)} %select_n.7), kind=kLoop, calls=%fused_computation.8 | loop fusion | bytes 262152 | tf_op jit(solution)/shard_map/jit(dynamic_index_in_dim)/squeeze | solution.py:45
  3.8 12.5 %collective-permute-done.10 = f32[128,128]{1,0:T(8,128)S(1)} collective-permute-done((f32[128,128]{1,0:T(8,128)S(1)}, f32[128,128]{1,0:T(8,128)S(1)}, u32[]{:S(2)}, u32[]{:S(2)}) %collective-permute-start.10) | collective-permute-done | bytes 65568 | tf_op jit(solution)/shard_map/ppermute | solution.py:41
  16.3 4.7 %collective-permute-start.12 = (f32[128,128]{1,0:T(8,128)S(1)}, f32[128,128]{1,0:T(8,128)S(1)}, u32[]{:S(2)}, u32[]{:S(2)}) collective-permute-start(f32[128,128]{1,0:T(8,128)S(1)} %collective-permute-done.10), channel_id=1, source_target_pairs={{0,8},{8,0},{4,12},{12,4},{1,9},{9,1},{5,13},{13,5},{2,10},{10,2},... | collective-permute-start | bytes 196616 | tf_op jit(solution)/shard_map/ppermute | solution.py:41
  21.0 1.7 %collective-permute-start = (f32[128,128]{1,0:T(8,128)S(1)}, f32[128,128]{1,0:T(8,128)S(1)}, u32[]{:S(2)}, u32[]{:S(2)}) collective-permute-start(f32[128,128]{1,0:T(8,128)S(1)} %get-tuple-element.36), channel_id=1, source_target_pairs={{0,16},{16,0},{1,17},{17,1},{2,18},{18,2},{3,19},{19,3},{4,20},{20... | collective-permute-start | bytes 196616 | tf_op jit(solution)/shard_map/ppermute | solution.py:41
  23.9 1.6 %collective-permute-start.14 = (f32[4,128,128]{2,1,0:T(8,128)S(1)}, f32[4,128,128]{2,1,0:T(8,128)S(1)}, u32[]{:S(2)}, u32[]{:S(2)}) collective-permute-start(f32[4,128,128]{2,1,0:T(8,128)S(1)} %pad_maximum_fusion.1.b_all), channel_id=1, source_target_pairs={{0,32},{32,0},{64,96},{96,64},{1,33},{33,1},{65,97},{97,65},{2,34}... | collective-permute-start | bytes 786440 | tf_op jit(solution)/shard_map/ppermute | solution.py:41
  26.1 3.0 %collective-permute-start.5 = (f32[128,128]{1,0:T(8,128)S(1)}, f32[128,128]{1,0:T(8,128)S(1)}, u32[]{:S(2)}, u32[]{:S(2)}) collective-permute-start(f32[128,128]{1,0:T(8,128)S(1)} %collective-permute-done.3), channel_id=1, source_target_pairs={{0,64},{64,0},{32,96},{96,32},{1,65},{65,1},{33,97},{97,33},{2,66}... | collective-permute-start | bytes 196616 | tf_op jit(solution)/shard_map/ppermute | solution.py:41
  29.1 1.1 %collective-permute-start.6 = (f32[128,128]{1,0:T(8,128)S(1)}, f32[128,128]{1,0:T(8,128)S(1)}, u32[]{:S(2)}, u32[]{:S(2)}) collective-permute-start(f32[128,128]{1,0:T(8,128)S(1)} %collective-permute-done.3), channel_id=1, source_target_pairs={{0,96},{96,0},{32,64},{64,32},{1,97},{97,1},{33,65},{65,33},{2,98}... | collective-permute-start | bytes 196616 | tf_op jit(solution)/shard_map/ppermute | solution.py:41
  30.2 4.3 %collective-permute-done.4 = f32[128,128]{1,0:T(8,128)S(1)} collective-permute-done((f32[128,128]{1,0:T(8,128)S(1)}, f32[128,128]{1,0:T(8,128)S(1)}, u32[]{:S(2)}, u32[]{:S(2)}) %collective-permute-start.4) | collective-permute-done | bytes 65568 | tf_op jit(solution)/shard_map/ppermute | solution.py:41
  34.6 2.9 %collective-permute-done.5 = f32[128,128]{1,0:T(8,128)S(1)} collective-permute-done((f32[128,128]{1,0:T(8,128)S(1)}, f32[128,128]{1,0:T(8,128)S(1)}, u32[]{:S(2)}, u32[]{:S(2)}) %collective-permute-start.5) | collective-permute-done | bytes 65568 | tf_op jit(solution)/shard_map/ppermute | solution.py:41
  38.3 2.1 %collective-permute-start.16 = (f32[4,128,128]{2,1,0:T(8,128)S(1)}, f32[4,128,128]{2,1,0:T(8,128)S(1)}, u32[]{:S(2)}, u32[]{:S(2)}) collective-permute-start(f32[4,128,128]{2,1,0:T(8,128)S(1)} %pad_maximum_fusion.1.b_all), channel_id=1, source_target_pairs={{0,96},{96,0},{32,64},{64,32},{1,97},{97,1},{33,65},{65,33},{2,98}... | collective-permute-start | bytes 786440 | tf_op jit(solution)/shard_map/ppermute | solution.py:41
  40.5 6.5 %collective-permute-start.8 = (f32[4,128,128]{2,1,0:T(8,128)S(1)}, f32[4,128,128]{2,1,0:T(8,128)S(1)}, u32[]{:S(2)}, u32[]{:S(2)}) collective-permute-start(f32[4,128,128]{2,1,0:T(8,128)S(1)} %pad_maximum_fusion.a_all), channel_id=1, source_target_pairs={{0,8},{8,0},{4,12},{12,4},{1,9},{9,1},{5,13},{13,5},{2,10},{10,2},... | collective-permute-start | bytes 786440 | tf_op jit(solution)/shard_map/ppermute | solution.py:41
  47.1 3.2 %shard_map.68 = (f32[2,16,128]{2,1,0:T(8,128)S(1)}, f32[1,1024]{1,0:T(1,128)}, f32[256,128]{1,0:T(8,128)S(1)}, f32[2,128,128]{2,1,0:T(8,128)S(1)}, bf16[512,512]...) custom-call(s32[2]{0:T(128)} %counts_hbm.1, ...), custom_call_target="tpu_custom_call" | custom-call | tf_op jit(solution)/shard_map/pallas_call | solution.py:68
  50.3 3.6 %collective-permute-start.18 = (f32[2,2,128,128]{3,2,1,0:T(8,128)S(1)}, f32[2,2,128,128]{3,2,1,0:T(8,128)S(1)}, u32[]{:S(2)}, u32[]{:S(2)}) collective-permute-start(f32[2,2,128,128]{3,2,1,0:T(8,128)S(1)} %pad_maximum_fusion.2), channel_id=1, source_target_pairs={{0,2},{2,0},{1,3},{3,1},{4,6},{6,4},{5,7},{7,5},{8,10},{10,8},{9,1... | collective-permute-start | bytes 786440 | tf_op jit(solution)/shard_map/ppermute | solution.py:41
  53.9 3.4 %collective-permute-done.8.a_far = f32[4,128,128]{2,1,0:T(8,128)S(1)} collective-permute-done((f32[4,128,128]{2,1,0:T(8,128)S(1)}, f32[4,128,128]{2,1,0:T(8,128)S(1)}, u32[]{:S(2)}, u32[]{:S(2)}) %collective-permute-start.8) | collective-permute-done | bytes 262176 | tf_op jit(solution)/shard_map/ppermute | solution.py:41
  57.4 2.6 %collective-permute-done.9.a_odd = f32[4,128,128]{2,1,0:T(8,128)S(1)} collective-permute-done((f32[4,128,128]{2,1,0:T(8,128)S(1)}, f32[4,128,128]{2,1,0:T(8,128)S(1)}, u32[]{:S(2)}, u32[]{:S(2)}) %collective-permute-start.9) | collective-permute-done | bytes 262176 | tf_op jit(solution)/shard_map/ppermute | solution.py:41
  59.9 1.6 %shard_map.69 = (f32[2,2,128,128]{3,2,1,0:T(8,128)S(1)}, f32[2,2,128,128]{3,2,1,0:T(8,128)S(1)}) custom-call(bf16[256,1024]{1,0:T(8,128)(2,1)S(1)} %get-tuple-element.16.band_hi, bf16[256,1024]{1,0:T(8,128)(2,1)S(1)} %get-tuple-element.17.band_lo, f32[4,128,128]{2,1,0:T(8,128)S(1)} %pad_maximum_fusion.a_all, ...), custom_call_target="tpu_custom_call" | custom-call | tf_op jit(solution)/shard_map/pallas_call | solution.py:68
  62.3 0.8 collective-permute-done.17.part_got
  63.1 1.2 %shard_map.71 = (f32[2,2,128,128]{3,2,1,0:T(8,128)S(1)}, f32[32,2,16,128]{3,2,1,0:T(8,128)}) custom-call(f32[2,2,128,128]{3,2,1,0:T(8,128)S(1)} %get-tuple-element.20.part_keep, f32[2,2,128,128]{3,2,1,0:T(8,128)S(1)} %collective-permute-done.17.part_got, bf16[512,256]{1,0:T(8,128)(2,1)S(1)} %get-tuple-element.24.left_hi, ...), custom_call_target="tpu_custom_call" | custom-call | tf_op jit(solution)/shard_map/pallas_call | solution.py:68
  64.3 6.8 %all-to-all-start = ((f32[64,16,128]{2,1,0:T(8,128)}), f32[64,16,128]{2,1,0:T(8,128)S(1)}, u32[]{:S(2)}, u32[]{:S(2)}) async-start(f32[64,16,128]{2,1,0:T(8,128)} %bitcast.17), calls=%async_computation | async-start | bytes 1048576 | tf_op jit(solution)/shard_map/all_to_all | solution.py:324
  71.1 3.2 %collective-permute-start.19 = (f32[128,128]{1,0:T(8,128)S(1)}, f32[128,128]{1,0:T(8,128)S(1)}, u32[]{:S(2)}, u32[]{:S(2)}) collective-permute-start(f32[128,128]{1,0:T(8,128)S(1)} %get-tuple-element.32), channel_id=1, source_target_pairs={{0,2},{2,0},{1,3},{3,1},{4,6},{6,4},{5,7},{7,5},{8,10},{10,8},{9,1... | collective-permute-start | bytes 196616 | tf_op jit(solution)/shard_map/ppermute | solution.py:41
  75.4 4.5 %collective-permute-done.19.in_a = f32[128,128]{1,0:T(8,128)S(1)} collective-permute-done((f32[128,128]{1,0:T(8,128)S(1)}, f32[128,128]{1,0:T(8,128)S(1)}, u32[]{:S(2)}, u32[]{:S(2)}) %collective-permute-start.19) | collective-permute-done | bytes 65568 | tf_op jit(solution)/shard_map/ppermute | solution.py:41
  79.9 2.7 %collective-permute-done.20.in_b = f32[128,128]{1,0:T(8,128)S(1)} collective-permute-done((f32[128,128]{1,0:T(8,128)S(1)}, f32[128,128]{1,0:T(8,128)S(1)}, u32[]{:S(2)}, u32[]{:S(2)}) %collective-permute-start.20) | collective-permute-done | bytes 65568 | tf_op jit(solution)/shard_map/ppermute | solution.py:41
  82.9 1.7 %all-to-all-done = f32[64,16,128]{2,1,0:T(8,128)S(1)} async-done(((f32[64,16,128]{2,1,0:T(8,128)}), f32[64,16,128]{2,1,0:T(8,128)S(1)}, u32[]{:S(2)}, u32[]{:S(2)}) %all-to-all-start) | async-done | bytes 524320 | tf_op jit(solution)/shard_map/all_to_all | solution.py:324
  (35 shorter events, 5.8 us)
Async XLA Ops:
  0.6 46.5 %copy-start = (f32[128,1024]{1,0:T(8,128)S(1)}, f32[128,1024]{1,0:T(8,128)}, u32[]{:S(2)}) copy-start(f32[128,1024]{1,0:T(8,128)} %band_own.1) | copy-start | bytes 1572868
  0.6 46.4 %collective-permute-start.2 = (f32[128,1024]{1,0:T(8,128)}, f32[128,1024]{1,0:T(8,128)S(1)}, u32[]{:S(2)}, u32[]{:S(2)}) collective-permute-start(f32[128,1024]{1,0:T(8,128)} %band_own.1), channel_id=1, source_target_pairs={{0,16},{16,0},{1,17},{17,1},{2,18},{18,2},{3,19},{19,3},{4,20},{20... | collective-permute-start | bytes 1572872 | tf_op jit(solution)/shard_map/ppermute | solution.py:41
  3.6 12.7 %collective-permute-start.10 = (f32[128,128]{1,0:T(8,128)S(1)}, f32[128,128]{1,0:T(8,128)S(1)}, u32[]{:S(2)}, u32[]{:S(2)}) collective-permute-start(f32[128,128]{1,0:T(8,128)S(1)} %get-tuple-element.36), channel_id=1, source_target_pairs={{0,16},{1,20},{2,24},{3,28},{4,17},{5,21},{6,25},{7,29},{8,18},{9,... | collective-permute-start | bytes 196616 | tf_op jit(solution)/shard_map/ppermute | solution.py:41
  16.3 6.4 %collective-permute-start.13 = (f32[128,128]{1,0:T(8,128)S(1)}, f32[128,128]{1,0:T(8,128)S(1)}, u32[]{:S(2)}, u32[]{:S(2)}) collective-permute-start(f32[128,128]{1,0:T(8,128)S(1)} %collective-permute-done.10), channel_id=1, source_target_pairs={{0,12},{12,0},{4,8},{8,4},{1,13},{13,1},{5,9},{9,5},{2,14},{14,2},... | collective-permute-start | bytes 196616 | tf_op jit(solution)/shard_map/ppermute | solution.py:41
  16.3 7.1 %collective-permute-start.11 = (f32[128,128]{1,0:T(8,128)S(1)}, f32[128,128]{1,0:T(8,128)S(1)}, u32[]{:S(2)}, u32[]{:S(2)}) collective-permute-start(f32[128,128]{1,0:T(8,128)S(1)} %collective-permute-done.10), channel_id=1, source_target_pairs={{0,4},{4,0},{8,12},{12,8},{1,5},{5,1},{9,13},{13,9},{2,6},{6,2},{1... | collective-permute-start | bytes 196616 | tf_op jit(solution)/shard_map/ppermute | solution.py:41
  16.3 7.6 %collective-permute-start.12 = (f32[128,128]{1,0:T(8,128)S(1)}, f32[128,128]{1,0:T(8,128)S(1)}, u32[]{:S(2)}, u32[]{:S(2)}) collective-permute-start(f32[128,128]{1,0:T(8,128)S(1)} %collective-permute-done.10), channel_id=1, source_target_pairs={{0,8},{8,0},{4,12},{12,4},{1,9},{9,1},{5,13},{13,5},{2,10},{10,2},... | collective-permute-start | bytes 196616 | tf_op jit(solution)/shard_map/ppermute | solution.py:41
  21.0 8.1 %collective-permute-start = (f32[128,128]{1,0:T(8,128)S(1)}, f32[128,128]{1,0:T(8,128)S(1)}, u32[]{:S(2)}, u32[]{:S(2)}) collective-permute-start(f32[128,128]{1,0:T(8,128)S(1)} %get-tuple-element.36), channel_id=1, source_target_pairs={{0,16},{16,0},{1,17},{17,1},{2,18},{18,2},{3,19},{19,3},{4,20},{20... | collective-permute-start | bytes 196616 | tf_op jit(solution)/shard_map/ppermute | solution.py:41
  22.7 2.8 %collective-permute-start.3 = (f32[128,128]{1,0:T(8,128)S(1)}, f32[128,128]{1,0:T(8,128)S(1)}, u32[]{:S(2)}, u32[]{:S(2)}) collective-permute-start(f32[128,128]{1,0:T(8,128)S(1)} %bitcast.26), channel_id=1, source_target_pairs={{0,0},{1,4},{2,8},{3,12},{4,1},{5,5},{6,9},{7,13},{8,2},{9,6},{10,... | collective-permute-start | bytes 196616 | tf_op jit(solution)/shard_map/ppermute | solution.py:41
  23.9 16.6 %collective-permute-start.14 = (f32[4,128,128]{2,1,0:T(8,128)S(1)}, f32[4,128,128]{2,1,0:T(8,128)S(1)}, u32[]{:S(2)}, u32[]{:S(2)}) collective-permute-start(f32[4,128,128]{2,1,0:T(8,128)S(1)} %pad_maximum_fusion.1.b_all), channel_id=1, source_target_pairs={{0,32},{32,0},{64,96},{96,64},{1,33},{33,1},{65,97},{97,65},{2,34}... | collective-permute-start | bytes 786440 | tf_op jit(solution)/shard_map/ppermute | solution.py:41
  25.5 9.1 %collective-permute-start.4 = (f32[128,128]{1,0:T(8,128)S(1)}, f32[128,128]{1,0:T(8,128)S(1)}, u32[]{:S(2)}, u32[]{:S(2)}) collective-permute-start(f32[128,128]{1,0:T(8,128)S(1)} %collective-permute-done.3), channel_id=1, source_target_pairs={{0,32},{32,0},{64,96},{96,64},{1,33},{33,1},{65,97},{97,65},{2,34}... | collective-permute-start | bytes 196616 | tf_op jit(solution)/shard_map/ppermute | solution.py:41
  26.1 11.4 %collective-permute-start.5 = (f32[128,128]{1,0:T(8,128)S(1)}, f32[128,128]{1,0:T(8,128)S(1)}, u32[]{:S(2)}, u32[]{:S(2)}) collective-permute-start(f32[128,128]{1,0:T(8,128)S(1)} %collective-permute-done.3), channel_id=1, source_target_pairs={{0,64},{64,0},{32,96},{96,32},{1,65},{65,1},{33,97},{97,33},{2,66}... | collective-permute-start | bytes 196616 | tf_op jit(solution)/shard_map/ppermute | solution.py:41
  29.1 9.2 %collective-permute-start.6 = (f32[128,128]{1,0:T(8,128)S(1)}, f32[128,128]{1,0:T(8,128)S(1)}, u32[]{:S(2)}, u32[]{:S(2)}) collective-permute-start(f32[128,128]{1,0:T(8,128)S(1)} %collective-permute-done.3), channel_id=1, source_target_pairs={{0,96},{96,0},{32,64},{64,32},{1,97},{97,1},{33,65},{65,33},{2,98}... | collective-permute-start | bytes 196616 | tf_op jit(solution)/shard_map/ppermute | solution.py:41
  34.6 5.8 %collective-permute-start.1 = (f32[2,128,128]{2,1,0:T(8,128)S(1)}, f32[2,128,128]{2,1,0:T(8,128)S(1)}, u32[]{:S(2)}, u32[]{:S(2)}) collective-permute-start(f32[2,128,128]{2,1,0:T(8,128)S(1)} %get-tuple-element.35), channel_id=1, source_target_pairs={{0,1},{1,0},{2,3},{3,2},{4,5},{5,4},{6,7},{7,6},{8,9},{9,8},{10,11... | collective-permute-start | bytes 393224 | tf_op jit(solution)/shard_map/ppermute | solution.py:41
  37.5 12.8 %collective-permute-start.15 = (f32[4,128,128]{2,1,0:T(8,128)S(1)}, f32[4,128,128]{2,1,0:T(8,128)S(1)}, u32[]{:S(2)}, u32[]{:S(2)}) collective-permute-start(f32[4,128,128]{2,1,0:T(8,128)S(1)} %pad_maximum_fusion.1.b_all), channel_id=1, source_target_pairs={{0,64},{64,0},{32,96},{96,32},{1,65},{65,1},{33,97},{97,33},{2,66}... | collective-permute-start | bytes 786440 | tf_op jit(solution)/shard_map/ppermute | solution.py:41
  38.3 15.6 %collective-permute-start.16 = (f32[4,128,128]{2,1,0:T(8,128)S(1)}, f32[4,128,128]{2,1,0:T(8,128)S(1)}, u32[]{:S(2)}, u32[]{:S(2)}) collective-permute-start(f32[4,128,128]{2,1,0:T(8,128)S(1)} %pad_maximum_fusion.1.b_all), channel_id=1, source_target_pairs={{0,96},{96,0},{32,64},{64,32},{1,97},{97,1},{33,65},{65,33},{2,98}... | collective-permute-start | bytes 786440 | tf_op jit(solution)/shard_map/ppermute | solution.py:41
  40.4 13.5 %collective-permute-start.7 = (f32[4,128,128]{2,1,0:T(8,128)S(1)}, f32[4,128,128]{2,1,0:T(8,128)S(1)}, u32[]{:S(2)}, u32[]{:S(2)}) collective-permute-start(f32[4,128,128]{2,1,0:T(8,128)S(1)} %pad_maximum_fusion.a_all), channel_id=1, source_target_pairs={{0,4},{4,0},{8,12},{12,8},{1,5},{5,1},{9,13},{13,9},{2,6},{6,2},{1... | collective-permute-start | bytes 786440 | tf_op jit(solution)/shard_map/ppermute | solution.py:41
  40.5 16.8 %collective-permute-start.8 = (f32[4,128,128]{2,1,0:T(8,128)S(1)}, f32[4,128,128]{2,1,0:T(8,128)S(1)}, u32[]{:S(2)}, u32[]{:S(2)}) collective-permute-start(f32[4,128,128]{2,1,0:T(8,128)S(1)} %pad_maximum_fusion.a_all), channel_id=1, source_target_pairs={{0,8},{8,0},{4,12},{12,4},{1,9},{9,1},{5,13},{13,5},{2,10},{10,2},... | collective-permute-start | bytes 786440 | tf_op jit(solution)/shard_map/ppermute | solution.py:41
  47.1 12.9 %collective-permute-start.9 = (f32[4,128,128]{2,1,0:T(8,128)S(1)}, f32[4,128,128]{2,1,0:T(8,128)S(1)}, u32[]{:S(2)}, u32[]{:S(2)}) collective-permute-start(f32[4,128,128]{2,1,0:T(8,128)S(1)} %pad_maximum_fusion.a_all), channel_id=1, source_target_pairs={{0,12},{12,0},{4,8},{8,4},{1,13},{13,1},{5,9},{9,5},{2,14},{14,2},... | collective-permute-start | bytes 786440 | tf_op jit(solution)/shard_map/ppermute | solution.py:41
  50.3 11.3 %collective-permute-start.18 = (f32[2,2,128,128]{3,2,1,0:T(8,128)S(1)}, f32[2,2,128,128]{3,2,1,0:T(8,128)S(1)}, u32[]{:S(2)}, u32[]{:S(2)}) collective-permute-start(f32[2,2,128,128]{3,2,1,0:T(8,128)S(1)} %pad_maximum_fusion.2), channel_id=1, source_target_pairs={{0,2},{2,0},{1,3},{3,1},{4,6},{6,4},{5,7},{7,5},{8,10},{10,8},{9,1... | collective-permute-start | bytes 786440 | tf_op jit(solution)/shard_map/ppermute | solution.py:41
  61.5 1.6 %collective-permute-start.17 = (f32[2,2,128,128]{3,2,1,0:T(8,128)S(1)}, f32[2,2,128,128]{3,2,1,0:T(8,128)S(1)}, u32[]{:S(2)}, u32[]{:S(2)}) collective-permute-start(f32[2,2,128,128]{3,2,1,0:T(8,128)S(1)} %get-tuple-element.21), channel_id=1, source_target_pairs={{0,1},{1,0},{2,3},{3,2},{4,5},{5,4},{6,7},{7,6},{8,9},{9,8},{10,11... | collective-permute-start | bytes 786440 | tf_op jit(solution)/shard_map/ppermute | solution.py:41
  64.3 20.3 %all-to-all-start = ((f32[64,16,128]{2,1,0:T(8,128)}), f32[64,16,128]{2,1,0:T(8,128)S(1)}, u32[]{:S(2)}, u32[]{:S(2)}) async-start(f32[64,16,128]{2,1,0:T(8,128)} %bitcast.17), calls=%async_computation | async-start | bytes 1048576 | tf_op jit(solution)/shard_map/all_to_all | solution.py:324
  71.1 8.8 %collective-permute-start.19 = (f32[128,128]{1,0:T(8,128)S(1)}, f32[128,128]{1,0:T(8,128)S(1)}, u32[]{:S(2)}, u32[]{:S(2)}) collective-permute-start(f32[128,128]{1,0:T(8,128)S(1)} %get-tuple-element.32), channel_id=1, source_target_pairs={{0,2},{2,0},{1,3},{3,1},{4,6},{6,4},{5,7},{7,5},{8,10},{10,8},{9,1... | collective-permute-start | bytes 196616 | tf_op jit(solution)/shard_map/ppermute | solution.py:41
  74.3 8.3 %collective-permute-start.20 = (f32[128,128]{1,0:T(8,128)S(1)}, f32[128,128]{1,0:T(8,128)S(1)}, u32[]{:S(2)}, u32[]{:S(2)}) collective-permute-start(f32[128,128]{1,0:T(8,128)S(1)} %get-tuple-element.31), channel_id=1, source_target_pairs={{0,16},{16,0},{1,17},{17,1},{2,18},{18,2},{3,19},{19,3},{4,20},{20... | collective-permute-start | bytes 196616 | tf_op jit(solution)/shard_map/ppermute | solution.py:41
  74.8 8.1 %collective-permute-start.21 = (f32[128,128]{1,0:T(8,128)S(1)}, f32[128,128]{1,0:T(8,128)S(1)}, u32[]{:S(2)}, u32[]{:S(2)}) collective-permute-start(f32[128,128]{1,0:T(8,128)S(1)} %get-tuple-element.30), channel_id=1, source_target_pairs={{0,18},{2,16},{16,2},{18,0},{1,19},{3,17},{17,3},{19,1},{4,22},{6,... | collective-permute-start | bytes 196616 | tf_op jit(solution)/shard_map/ppermute | solution.py:41
